TPU v7x, 32 devices: a whole 2x2x4 slice. The times are simulated.
32 devices in a mesh: orient: 8 (over z, y), brow: 2 (over core), bcol: 2 (over x).
Axes of the slice: x: 2, y: 2, z: 4, core: 2. Of those that a mesh axis runs over, the one named last changes fastest.
Arguments:
- volume: float32 [8, 64, 208], P('orient', 'brow', 'bcol'), may hold values from -700 to 700
- template: float32 [24, 24, 24], replicated, may hold values from 0 to 1
- voxel_maps: int32 [8, 13824], P('orient'), may hold values from 0 to 13823, as said below
Outputs:
- best: float32 [8, 64, 208], P('orient', 'brow', 'bcol')
Inputs may be any that keep to these rules, and one draw needn't show every extreme that they name: `voxel_maps`: each row holds every number of 0 to 13823 exactly once.
All inputs are finite; a program needn't handle non-finite values.
Results may differ from a plain program's by a relative error of at most 0.00013.
Values sent between devices are 32-bit elements; how exact they have to be, the bound alone decides.
A program may use at most 64 MiB of HBM per device.

v0:
```python
import math

import numpy as np
import jax
import jax.numpy as jnp
from jax import lax
from jax.experimental import pallas as pl
from jax.experimental.pallas import tpu as pltpu
from jax.sharding import PartitionSpec as P

epsilon = 1e-06
floor_share = 0.1
highest = lax.Precision.HIGHEST
LANES = 128
MESH = pl.DeviceIdType.MESH


def round_up(value, step):
    return -(-value // step) * step


def forward_table(length, parts):
    half = length // 2 + 1
    padded = round_up(half, LANES)
    angles = 2.0 * np.pi * (np.outer(np.arange(length), np.arange(half)) % length) / length
    table = np.zeros((length, 2 * padded))
    table[:, :half] = np.cos(angles)
    table[:, padded : padded + half] = -np.sin(angles)
    return table.reshape(parts, length // parts, 2 * padded).astype(np.float32)


def smoothing_table(length):
    half = length // 2 + 1
    padded = round_up(half, LANES)
    table = np.zeros((padded, padded))
    fold = np.minimum(np.arange(length), length - np.arange(length))
    for k in range(half):
        for shift in (-1, 0, 1):
            table[fold[(k + shift) % length], k] += 1.0 / 3.0
        for other in range(length):
            table[fold[other], k] += floor_share / length
    return table.astype(np.float32)


def windowed_inverse(length, parts, margin):
    half = length // 2 + 1
    padded = round_up(half, LANES)
    width = length // parts
    tables = np.zeros((parts, 2 * padded, width + 2 * margin))
    k = np.arange(half)
    share = np.where((k == 0) | (2 * k == length), 1.0, 2.0)[:, None] / math.sqrt(length)
    for part in range(parts):
        columns = np.arange(width + 2 * margin) + part * width - margin
        inside = (columns >= 0) & (columns < length)
        angles = 2.0 * np.pi * (np.outer(k, columns) % length) / length
        tables[part, :half] = share * np.cos(angles) * inside
        tables[part, padded : padded + half] = -share * np.sin(angles) * inside
    return tables.astype(np.float32)


def packed_dft(count, size):
    k = np.arange(size)
    real = k <= size // 2
    freq = np.where(real, k, k - size // 2)
    angles = 2.0 * np.pi * (np.outer(np.arange(count), freq) % size) / size
    return angles, real, freq


def volume_table(size):
    angles, real, freq = packed_dft(size, size)
    return np.where(real, np.cos(angles), -np.sin(angles)).astype(np.float32)


def template_table(count, size):
    angles, real, freq = packed_dft(count, size)
    straight = np.cos(angles)
    edge = (freq == 0) | (freq == size // 2)
    crossed = np.where(real, -np.sin(angles), np.sin(angles)) * ~edge
    return np.concatenate([straight, crossed], axis=1).astype(np.float32)


def score_table(size, count):
    angles, real, freq = packed_dft(count, size)
    share = np.where((freq == 0) | (freq == size // 2), 1.0, 2.0)
    return (np.where(real, np.cos(angles), -np.sin(angles)) * share / size).T.astype(np.float32)


def box_table(size, count, edge):
    offsets = np.arange(size)[:, None] - np.arange(count)[None, :]
    return ((offsets >= 0) & (offsets < edge)).astype(np.float32)


def dot(a, b):
    return jnp.dot(a, b, precision=highest, preferred_element_type=jnp.float32)


def split_table(template_ref, normed):
    lines, edge = template_ref.shape
    template = template_ref[...]
    centred = template - jnp.sum(template, keepdims=True) / (lines * edge)
    normed[...] = centred / jnp.sqrt(jnp.sum(centred * centred, keepdims=True) + epsilon)
    table = jnp.concatenate([normed[pl.ds(j, lines // 8, stride=8), :] for j in range(8)], axis=1)
    spare = round_up(lines // 8, 16) - lines // 8
    table = jnp.concatenate([table, jnp.zeros((spare, 8 * edge), jnp.float32)], axis=0)
    upper = table.astype(jnp.bfloat16)
    lower = (table - upper.astype(jnp.float32)).astype(jnp.bfloat16)
    return jnp.concatenate([upper, lower], axis=0)


def look_up(pieces, index):
    count, span = pieces.shape
    width = index.shape[1]
    high = ((index.astype(jnp.float32) + 0.5) * (1.0 / span)).astype(jnp.int32)
    low = index - high * span
    chosen = lax.broadcasted_iota(jnp.int32, (span, width), 0) == low
    lanes = jnp.dot(
        pieces,
        jnp.where(chosen, 1.0, 0.0).astype(jnp.bfloat16),
        preferred_element_type=jnp.float32,
    )
    lanes = lanes[: count // 2] + lanes[count // 2 :]
    mine = lax.broadcasted_iota(jnp.int32, lanes.shape, 0) == high
    return jnp.sum(jnp.where(mine, lanes, 0.0), axis=0, keepdims=True)


def match_kernel(
    sizes,
    fetch,
    brick_ref,
    template_ref,
    index_ref,
    template_dft_ref,
    forward_ref,
    smoothing_ref,
    inverse_ref,
    volume_dft_ref,
    score_dft_ref,
    box_ref,
    best_ref,
    scaling_ref,
    normed,
    rotated,
    rotations,
    straight_ref,
    crossed_ref,
    pencils,
    tall,
    windows,
    spectrum,
    swapped,
    energy,
    totals,
    sems0,
    sems1,
    sems2,
):
    orients, brows, bcols, edge, voxels, base, first, last = sizes
    half_edge = edge // 2
    rows, cols = brick_ref.shape[1:]
    tile_rows = windows.shape[1]
    me = lax.axis_index("orient")
    row_id = lax.axis_index("brow")
    col_id = lax.axis_index("bcol")
    group = brows * bcols
    place = row_id * bcols + col_id

    def brick_peer(step):
        other = lax.rem(place + step, group)
        return {"orient": me, "brow": other // bcols, "bcol": lax.rem(other, bcols)}

    def partner(step):
        assert orients & (orients - 1) == 0
        other, weight = 0, 1
        while weight < orients:
            other = other + lax.rem(me // weight + step // weight, 2) * weight
            weight *= 2
        return other

    def plane_peer(step):
        return {"orient": partner(step), "brow": row_id, "bcol": col_id}

    windows[...] = jnp.zeros_like(windows)
    barrier = pltpu.get_barrier_semaphore()
    for step in range(1, group):
        pl.semaphore_signal(barrier, inc=1, device_id=brick_peer(step), device_id_type=MESH)
    for step in range(1, orients):
        pl.semaphore_signal(barrier, inc=1, device_id=plane_peer(step), device_id_type=MESH)

    fetch()
    energy[...] = jnp.zeros_like(energy)
    totals[...] = jnp.zeros_like(totals)
    tall[...] = jnp.zeros_like(tall)
    if first > base or last < base + rotated.shape[0]:
        rotated[...] = jnp.zeros_like(rotated)
    pieces = split_table(template_ref, normed)

    pl.semaphore_wait(barrier, group + orients - 2)

    gathers = []
    for step in range(1, group):
        copy = pltpu.make_async_remote_copy(
            src_ref=brick_ref.at[0],
            dst_ref=pencils.at[col_id, row_id],
            send_sem=sems1.at[0, step],
            recv_sem=sems1.at[1, step],
            device_id=brick_peer(step),
            device_id_type=MESH,
        )
        copy.start()
        gathers.append(copy)
    pencils[col_id, row_id] = brick_ref[0]
    plane_voxels = edge * edge

    @pl.loop(0, (last - first) // 2)
    def _(pair):
        start = pl.multiple_of((first + 2 * pair) * plane_voxels, 2 * plane_voxels)
        found = look_up(pieces, index_ref[0:1, pl.ds(start, 2 * plane_voxels)])
        for i in range(2):
            rotated[first - base + 2 * pair + i] = found[:, i * plane_voxels : (i + 1) * plane_voxels]

    rotations[me] = rotated[pl.ds(half_edge - me - base, orients)]
    parts = brows if orients % brows == 0 else 1
    part_planes = orients // parts
    shares = []
    for step in range(1, orients):
        target = partner(step)
        copy = pltpu.make_async_remote_copy(
            src_ref=rotated.at[pl.ds(half_edge - target - base + lax.rem(row_id, parts) * part_planes, part_planes)],
            dst_ref=rotations.at[me, pl.ds(lax.rem(row_id, parts) * part_planes, part_planes)],
            send_sem=sems0.at[0, 0, step],
            recv_sem=sems0.at[0, 1, step],
            device_id=plane_peer(step),
            device_id_type=MESH,
        )
        copy.start()
        shares.append(copy)
    for copy in gathers:
        copy.wait_recv()

    both = None
    for part in range(bcols):
        term = dot(pencils[part].reshape(brows * rows, cols), forward_ref[part])
        both = term if both is None else both + term
    padded = both.shape[1] // 2
    real, imag = both[:, :padded], both[:, padded:]
    weights = lax.rsqrt(dot(real * real + imag * imag, smoothing_ref[...]) + epsilon)
    tall[half_edge : half_edge + brows * rows, :] = dot(
        real * weights, inverse_ref[col_id, :padded, :]
    ) + dot(imag * weights, inverse_ref[col_id, padded:, :])
    start = pl.multiple_of(row_id * rows, 8)
    windows[me] = tall[pl.ds(start, tile_rows), :]
    idle = half_edge // 8 * 8 if brows == 2 else 0
    filled = pl.ds(pl.multiple_of((brows - 1 - row_id) * idle, 8), tile_rows - idle)

    sends = []
    for step in range(1, orients):
        copy = pltpu.make_async_remote_copy(
            src_ref=windows.at[me, filled],
            dst_ref=windows.at[me, filled],
            send_sem=sems2.at[0, step],
            recv_sem=sems2.at[1, step],
            device_id=plane_peer(step),
            device_id_type=MESH,
        )
        copy.start()
        sends.append(copy)

    def unfold(rotation):
        planes = rotations[rotation][:, 0, :]
        lines = jnp.concatenate(
            [planes[:, b * edge : (b + 1) * edge] for b in range(edge)], axis=0
        )
        turned = dot_short(lines, template_dft_ref[...])
        size = turned.shape[1] // 2
        straight_ref[rotation] = turned[:, :size].reshape(edge, orients, size)
        crossed_ref[rotation] = turned[:, size:].reshape(edge, orients, size)

    unfold(me)

    def share_of(step, turn):
        source = partner(step)
        owner = lax.rem(row_id, parts) * part_planes
        block = rotations.at[source, pl.ds(owner, part_planes)]
        to = plane_peer(step)
        if turn:
            to = {"orient": me, "brow": lax.rem(row_id + turn, brows), "bcol": col_id}
        return pltpu.make_async_remote_copy(
            src_ref=block,
            dst_ref=block,
            send_sem=sems0.at[turn, 0, step],
            recv_sem=sems0.at[turn, 1, step],
            device_id=to,
            device_id_type=MESH,
        )

    @pl.loop(1, orients)
    def _(step):
        share_of(step, 0).wait_recv()
        for turn in range(1, parts):
            share_of(step, turn).start()

    @pl.loop(1, orients)
    def _(step):
        for turn in range(1, parts):
            share_of(step, turn).wait()
        unfold(partner(step))

    bunch = math.gcd(orients, 8)

    def absorb(plane):
        window = windows[plane]
        gap = plane - me
        near = jnp.logical_and(gap >= -half_edge, gap < half_edge).astype(jnp.float32)
        energy[...] += window * window * near
        transformed = dot_short(window, volume_dft_ref[...])
        spectrum[...] = transformed
        swapped[...] = pltpu.roll(transformed, transformed.shape[1] // 2, 1)

        def targets(piece):
            lowest = piece * bunch
            held = [totals[lowest + r] for r in range(bunch)]
            for b in range(edge):
                near_part = spectrum[b : b + rows, :]
                far_part = swapped[b : b + rows, :]
                for r in range(bunch):
                    held[r] = held[r] + (
                        near_part * straight_ref[lowest + r, b, pl.ds(plane, 1), :]
                        + far_part * crossed_ref[lowest + r, b, pl.ds(plane, 1), :]
                    )
            for r in range(bunch):
                totals[lowest + r] = held[r]

        if orients == bunch:
            targets(0)
        else:
            pl.loop(0, orients // bunch)(targets)

    absorb(me)

    @pl.loop(1, orients)
    def _(step):
        source = partner(step)
        pltpu.make_async_remote_copy(
            src_ref=windows.at[source, filled],
            dst_ref=windows.at[source, filled],
            send_sem=sems2.at[0, step],
            recv_sem=sems2.at[1, step],
            device_id=plane_peer(step),
            device_id_type=MESH,
        ).wait_recv()
        absorb(source)

    summed = energy[0:rows, :]
    for b in range(1, edge):
        summed = summed + energy[b : b + rows, :]
    scaling = lax.rsqrt(dot(summed, box_ref[...]) / voxels + epsilon)
    size = spectrum.shape[1]
    scored = dot_short(totals[...].reshape(orients * rows, size), score_dft_ref[...])
    best = jnp.max(scored.reshape(orients, rows, cols), axis=0)
    best_ref[0] = best
    scaling_ref[0] = scaling
    for copy in gathers + shares + sends:
        copy.wait_send()


def dot_short(a, b):
    return jnp.dot(a, b, precision=lax.Precision.HIGH, preferred_element_type=jnp.float32)


def staged(sizes, count, *refs):
    sources, results = refs[:count], refs[count : count + 2]
    held, rest = refs[count + 2 : 2 * count + 2], refs[2 * count + 2 : -1]
    copies = [
        pltpu.make_async_copy(source, target, refs[-1].at[i])
        for i, (source, target) in enumerate(zip(sources, held))
    ]
    for copy in copies:
        copy.start()

    def fetch():
        for copy in copies:
            copy.wait()

    match_kernel(sizes, fetch, *held, *results, *rest)


def shards(volume, template, voxel_maps):
    orients, brows, bcols = (lax.axis_size(axis) for axis in ("orient", "brow", "bcol"))
    planes, rows, cols = volume.shape
    edge = template.shape[0]
    half_edge = edge // 2
    voxels = edge**3
    length = cols * bcols
    size = cols + edge
    tile_rows = rows + edge
    base = (half_edge - orients + 1) // 2 * 2
    first = max(0, base)
    last = min(edge, round_up(half_edge + orients, 2))
    held = round_up(half_edge + orients, 2) - base
    group = brows * bcols
    vmem = pl.BlockSpec(memory_space=pltpu.VMEM)
    constants = (
        template_table(edge, size),
        forward_table(length, bcols),
        smoothing_table(length),
        windowed_inverse(length, bcols, half_edge),
        volume_table(size),
        score_table(size, cols),
        box_table(size, cols, edge),
    )
    sizes = (orients, brows, bcols, edge, voxels, base, first, last)
    operands = (volume, template.reshape(edge * edge, edge), voxel_maps)
    operands += tuple(jnp.asarray(c) for c in constants)
    best, scaling = pl.pallas_call(
        lambda *refs: staged(sizes, len(operands), *refs),
        out_shape=(jax.ShapeDtypeStruct((1, rows, cols), jnp.float32),) * 2,
        in_specs=[pl.BlockSpec(memory_space=pl.ANY)] * len(operands),
        out_specs=(vmem, vmem),
        scratch_shapes=[pltpu.VMEM(x.shape, x.dtype) for x in operands]
        + [
            pltpu.VMEM((edge * edge, edge), jnp.float32),
            pltpu.VMEM((held, 1, edge * edge), jnp.float32),
            pltpu.VMEM((orients, orients, 1, edge * edge), jnp.float32),
            pltpu.VMEM((orients, edge, orients, size), jnp.float32),
            pltpu.VMEM((orients, edge, orients, size), jnp.float32),
            pltpu.VMEM((bcols, brows, rows, cols), jnp.float32),
            pltpu.VMEM((brows * rows + edge, size), jnp.float32),
            pltpu.VMEM((orients, tile_rows, size), jnp.float32),
            pltpu.VMEM((tile_rows, size), jnp.float32),
            pltpu.VMEM((tile_rows, size), jnp.float32),
            pltpu.VMEM((tile_rows, size), jnp.float32),
            pltpu.VMEM((orients, rows, size), jnp.float32),
            pltpu.SemaphoreType.DMA((brows, 2, orients)),
            pltpu.SemaphoreType.DMA((2, group)),
            pltpu.SemaphoreType.DMA((2, orients)),
            pltpu.SemaphoreType.DMA((len(operands),)),
        ],
        compiler_params=pltpu.CompilerParams(collective_id=0, has_side_effects=True),
        name="match",
    )(*operands)
    return best * scaling


def solution(mesh):
    in_specs = (P("orient", "brow", "bcol"), P(), P("orient", None))
    out_specs = P("orient", "brow", "bcol")
    return jax.shard_map(shards, mesh=mesh, in_specs=in_specs, out_specs=out_specs, check_vma=False)
```

profile of v0, /device:TPU:0, one launch (start us, length us, event | category | flops | bytes accessed | tf_op | source)
XLA Modules:
  0.0 23.7 jit_solution(17670498551316499539)
XLA Ops:
  0.0 22.4 %match.1 = (f32[1,32,104]{2,1,0:T(8,128)}, f32[1,32,104]{2,1,0:T(8,128)}) custom-call(f32[1,32,104]{2,1,0:T(8,128)} %refs_0_.1, f32[576,24]{1,0:T(8,128)} %bitcast.1, s32[1,13824]{1,0:T(1,128)} %refs_2_.1, f32[24,256]{1,0:T(8,128)} %constant.14.clone.refs_3_, f32[2,104,256]{2,1,0:T(8,128)} %constant.15.clone.refs_4_, f32[128,128]{1,0:T(8,128)} %constant.16.clone.refs_5_, ...), custom_call_target="tpu_custom_call" | custom-call | tf_op jit(solution)/shard_map/match/pallas_call | solution.py:414
  22.4 1.3 %mul.3 = f32[1,32,104]{2,1,0:T(8,128)} multiply(f32[1,32,104]{2,1,0:T(8,128)} %get-tuple-element.7, f32[1,32,104]{2,1,0:T(8,128)} %get-tuple-element.8) | non-fusion elementwise | flops 3328 | bytes 39936 | tf_op jit(solution)/shard_map/mul | solution.py:441
where the time goes:
time: 24.1 us; the launch traced here: 23.7 us
  Pallas kernels  22.4 us (93%)
  other arithmetic  1.34 us (6%)
    pallas_call x1, Pallas kernels, shards(): pl.pallas_call(lambda *refs: staged(sizes, len(operands), *refs), out_sha...  22.4 us
    mul x1, other arithmetic, shards(): return best * scaling  1.34 us

commit v1 on v0

--- a/solution.py
+++ b/solution.py
@@ -413,7 +413,7 @@
     operands += tuple(jnp.asarray(c) for c in constants)
     best, scaling = pl.pallas_call(
         lambda *refs: staged(sizes, len(operands), *refs),
-        out_shape=(jax.ShapeDtypeStruct((1, rows, cols), jnp.float32),) * 2,
+        out_shape=(pltpu.VMEM((1, rows, cols), jnp.float32),) * 2,
         in_specs=[pl.BlockSpec(memory_space=pl.ANY)] * len(operands),
         out_specs=(vmem, vmem),
         scratch_shapes=[pltpu.VMEM(x.shape, x.dtype) for x in operands]

time: 24.1 us -> 22.6 us (0.938)
  other arithmetic: 1.34 us -> 0.61 us
  Pallas kernels: 22.4 us -> 21.8 us
    mul x1, other arithmetic: 1.34 us -> 0.61 us  [shards(): return best * scaling]
    pallas_call x1, Pallas kernels: 22.4 us -> 21.8 us  [shards(): pl.pallas_call(lambda *refs: staged(sizes, len(operands), *refs), out_sha...]
where the time goes in v1:
time: 22.6 us; the launch traced here: 22.4 us
  Pallas kernels  21.8 us (96%)
  other arithmetic  0.61 us (3%)
    pallas_call x1, Pallas kernels, shards(): pl.pallas_call(lambda *refs: staged(sizes, len(operands), *refs), out_sha...  21.8 us
    mul x1, other arithmetic, shards(): return best * scaling  0.61 us

profile of v1, /device:TPU:0, one launch (start us, length us, event | category | flops | bytes accessed | tf_op | source)
XLA Modules:
  0.0 22.4 jit_solution(12712071534947765392)
XLA Ops:
  0.0 21.8 %match.1 = (f32[1,32,104]{2,1,0:T(8,128)S(1)}, f32[1,32,104]{2,1,0:T(8,128)S(1)}) custom-call(f32[1,32,104]{2,1,0:T(8,128)} %refs_0_.1, f32[576,24]{1,0:T(8,128)} %bitcast.1, s32[1,13824]{1,0:T(1,128)} %refs_2_.1, f32[24,256]{1,0:T(8,128)} %constant.14.clone.refs_3_, f32[2,104,256]{2,1,0:T(8,128)} %constant.15.clone.refs_4_, ...), custom_call_target="tpu_custom_call" | custom-call | tf_op jit(solution)/shard_map/match/pallas_call | solution.py:414
  21.8 0.6 %mul.3 = f32[1,32,104]{2,1,0:T(8,128)} multiply(f32[1,32,104]{2,1,0:T(8,128)S(1)} %get-tuple-element.7, f32[1,32,104]{2,1,0:T(8,128)S(1)} %get-tuple-element.8) | non-fusion elementwise | flops 3328 | bytes 39936 | tf_op jit(solution)/shard_map/mul | solution.py:441

commit v2 on v1

v2 whole, which is shorter than its diff:
```python
import math

import numpy as np
import jax
import jax.numpy as jnp
from jax import lax
from jax.experimental import pallas as pl
from jax.experimental.pallas import tpu as pltpu
from jax.sharding import PartitionSpec as P

epsilon = 1e-06
floor_share = 0.1
LANES = 128
MESH = pl.DeviceIdType.MESH


def round_up(value, step):
    return -(-value // step) * step


def forward_table(length, parts):
    half = length // 2 + 1
    padded = round_up(half, LANES)
    angles = 2.0 * np.pi * (np.outer(np.arange(length), np.arange(half)) % length) / length
    table = np.zeros((length, 2 * padded))
    table[:, :half] = np.cos(angles)
    table[:, padded : padded + half] = -np.sin(angles)
    return table.reshape(parts, length // parts, 2 * padded).astype(np.float32)


def smoothing_table(length):
    half = length // 2 + 1
    padded = round_up(half, LANES)
    table = np.zeros((padded, padded))
    fold = np.minimum(np.arange(length), length - np.arange(length))
    for k in range(half):
        for shift in (-1, 0, 1):
            table[fold[(k + shift) % length], k] += 1.0 / 3.0
        for other in range(length):
            table[fold[other], k] += floor_share / length
    return table.astype(np.float32)


def windowed_inverse(length, parts, margin):
    half = length // 2 + 1
    padded = round_up(half, LANES)
    width = length // parts
    tables = np.zeros((parts, 2 * padded, width + 2 * margin))
    k = np.arange(half)
    share = np.where((k == 0) | (2 * k == length), 1.0, 2.0)[:, None] / math.sqrt(length)
    for part in range(parts):
        columns = np.arange(width + 2 * margin) + part * width - margin
        inside = (columns >= 0) & (columns < length)
        angles = 2.0 * np.pi * (np.outer(k, columns) % length) / length
        tables[part, :half] = share * np.cos(angles) * inside
        tables[part, padded : padded + half] = -share * np.sin(angles) * inside
    return tables.astype(np.float32)


def split(table):
    upper = table.astype(jnp.bfloat16)
    lower = (table - upper.astype(np.float64)).astype(jnp.bfloat16)
    return upper, lower


def left_table(table):
    upper, lower = split(table)
    return np.concatenate([upper, lower, upper], axis=1)


def right_table(table):
    upper, lower = split(table)
    return np.concatenate([upper, upper, lower], axis=0)


def odd_waves(count, size):
    angles = np.pi * (np.outer(np.arange(count), 2 * np.arange(size // 2) + 1) % (2 * size)) / size
    return np.cos(angles), np.sin(angles)


def line_table(count, size):
    cos, sin = odd_waves(count, size)
    return np.concatenate([cos, -sin, -sin, -cos], axis=1)


def row_waves(size, count):
    angles = 2.0 * np.pi * (np.outer(np.arange(size), np.arange(count)) % size) / size
    return np.cos(angles), np.sin(angles)


def template_lines(edge, size, strips):
    span = edge // strips
    waves = line_table(edge, size)
    table = np.zeros((LANES, 2, span, size))
    for b in range(span):
        for half in range(2):
            table[b * edge : (b + 1) * edge, half, b] = waves[:, half * size : (half + 1) * size]
    return right_table(table.reshape(LANES, -1))


def template_rows(size, edge, strips):
    order = np.arange(edge).reshape(strips, edge // strips).T.reshape(-1)
    return left_table(np.concatenate([wave[:, order] for wave in row_waves(size, edge)], axis=1))


def volume_rows(size):
    cos, sin = row_waves(size, size)
    return left_table(np.block([[cos, sin], [-sin, cos]]))


def score_rows(size, rows):
    cos, sin = (wave.T / size for wave in row_waves(size, rows))
    return left_table(np.block([[cos, -sin], [sin, cos]]))


def score_lines(size, count):
    cos, sin = (wave.T * (2.0 / size) for wave in odd_waves(count, size))
    return right_table(np.concatenate([cos, cos, -sin, -sin], axis=0))


def box_table(size, count, edge):
    offsets = np.arange(size)[:, None] - np.arange(count)[None, :]
    return ((offsets >= 0) & (offsets < edge)).astype(jnp.bfloat16)


def split_table(template_ref, normed):
    lines, edge = template_ref.shape
    template = template_ref[...]
    centred = template - jnp.sum(template, keepdims=True) / (lines * edge)
    normed[...] = centred / jnp.sqrt(jnp.sum(centred * centred, keepdims=True) + epsilon)
    table = jnp.concatenate([normed[pl.ds(j, lines // 8, stride=8), :] for j in range(8)], axis=1)
    spare = round_up(lines // 8, 16) - lines // 8
    table = jnp.concatenate([table, jnp.zeros((spare, 8 * edge), jnp.float32)], axis=0)
    upper = table.astype(jnp.bfloat16)
    lower = (table - upper.astype(jnp.float32)).astype(jnp.bfloat16)
    return jnp.concatenate([upper, lower], axis=0)


def look_up(pieces, index):
    count, span = pieces.shape
    width = index.shape[1]
    high = ((index.astype(jnp.float32) + 0.5) * (1.0 / span)).astype(jnp.int32)
    low = index - high * span
    chosen = lax.broadcasted_iota(jnp.int32, (span, width), 0) == low
    lanes = jnp.dot(
        pieces,
        jnp.where(chosen, 1.0, 0.0).astype(jnp.bfloat16),
        preferred_element_type=jnp.float32,
    )
    lanes = lanes[: count // 2] + lanes[count // 2 :]
    mine = lax.broadcasted_iota(jnp.int32, lanes.shape, 0) == high
    return jnp.sum(jnp.where(mine, lanes, 0.0), axis=0, keepdims=True)


def halves(x):
    upper = x.astype(jnp.bfloat16)
    return upper, (x - upper.astype(jnp.float32)).astype(jnp.bfloat16)


def product(a, b):
    return jnp.dot(a, b, preferred_element_type=jnp.float32)


def by_table(x, table):
    upper, lower = halves(x)
    return product(jnp.concatenate([upper, lower, upper], axis=1), table)


def table_by(table, x):
    upper, lower = halves(x)
    return product(table, jnp.concatenate([upper, upper, lower], axis=0))


def match_kernel(
    sizes,
    refs,
    copies,
    rotated,
    rotations,
    lines,
    templates,
    volumes,
    pencils,
    windows,
    energy,
    scores,
    normed,
    own_sem,
    gather_sems,
    share_sems,
    turn_sems,
    window_sems,
    send_sems,
    best_ref,
    scaling_ref,
):
    orients, brows, bcols, parts, edge, base, margin, batch, strips = sizes
    half_edge = edge // 2
    rows, cols = refs["brick"].shape[1:]
    tile_rows, size = energy.shape
    skip = margin - half_edge
    me = lax.axis_index("orient")
    row_id = lax.axis_index("brow")
    col_id = lax.axis_index("bcol")
    share = orients // parts
    mine = lax.rem(row_id, parts)
    plane_voxels = edge * edge
    span = edge // strips

    def column_peer(step):
        return {"orient": me, "brow": row_id, "bcol": lax.rem(col_id + step, bcols)}

    def partner(step):
        assert orients & (orients - 1) == 0
        other, weight = 0, 1
        while weight < orients:
            other = other + lax.rem(me // weight + step // weight, 2) * weight
            weight *= 2
        return other

    partners = [partner(step) for step in range(orients)]

    def plane_peer(step, turn=0):
        return {"orient": partners[step], "brow": lax.rem(row_id + turn, brows), "bcol": col_id}

    def first_of(part, plane):
        start = orients - plane
        rest = lax.rem(start, 2 * parts) + 2 * parts - 2 * part
        return start // (2 * parts) * 2 + (rest - 1) // (2 * parts) + (rest - 2) // (2 * parts)

    def plane_of(slot):
        part, index = slot // share, slot % share
        found = first_of(part, me) + index
        return found // 2 * (2 * parts) + 2 * part + lax.rem(found, 2) - orients + me

    windows[...] = jnp.zeros_like(windows)
    barrier = pltpu.get_barrier_semaphore()
    for step in range(1, bcols):
        pl.semaphore_signal(barrier, inc=1, device_id=column_peer(step), device_id_type=MESH)
    for step in range(orients):
        for turn in range(brows):
            if step or turn:
                pl.semaphore_signal(barrier, inc=1, device_id=plane_peer(step, turn), device_id_type=MESH)
    for copy in copies.values():
        copy.start()
    own = pltpu.make_async_copy(refs["brick"].at[0], pencils.at[col_id], own_sem)
    own.start()
    energy[...] = jnp.zeros_like(energy)
    rotated[...] = jnp.zeros_like(rotated)
    planes_of = [plane_of(slot) for slot in range(orients)]
    pl.semaphore_wait(barrier, bcols - 1 + orients * brows - 1)

    def gather_of(step, place):
        return pltpu.make_async_remote_copy(
            src_ref=refs["brick"].at[0],
            dst_ref=pencils.at[place],
            send_sem=send_sems.at[0],
            recv_sem=gather_sems.at[step],
            device_id=column_peer(step),
            device_id_type=MESH,
        )

    for step in range(1, bcols):
        gather_of(step, col_id).start()

    copies["template"].wait()
    pieces = split_table(refs["template"], normed)
    copies["index"].wait()

    @pl.loop(0, orients // parts)
    def _(pair):
        plane = base + 2 * mine + 2 * parts * pair

        def fill():
            start = pl.multiple_of(plane * plane_voxels, 2 * plane_voxels)
            found = look_up(pieces, refs["index"][0:1, pl.ds(start, 2 * plane_voxels)])
            for i in range(2):
                rotated[2 * pair + i, :, :plane_voxels] = found[:, i * plane_voxels : (i + 1) * plane_voxels]

        if base < 0 or base + 2 * orients > edge:
            pl.when(jnp.logical_and(plane >= 0, plane < edge))(fill)
        else:
            fill()

    def block(rotation, part):
        return rotations.at[rotation, pl.ds(part * share, share)]

    def share_of(step, rotation):
        return pltpu.make_async_remote_copy(
            src_ref=rotated.at[pl.ds(first_of(mine, partners[step]), share)],
            dst_ref=block(rotation, mine),
            send_sem=send_sems.at[1],
            recv_sem=share_sems.at[step],
            device_id=plane_peer(step),
            device_id_type=MESH,
        )

    def turn_of(step, turn):
        return pltpu.make_async_remote_copy(
            src_ref=block(partners[step], mine),
            dst_ref=block(partners[step], mine),
            send_sem=send_sems.at[2],
            recv_sem=turn_sems.at[step],
            device_id=plane_peer(0, turn),
            device_id_type=MESH,
        )

    for step in reversed(range(1, orients)):
        share_of(step, me).start()
    rotations[me, pl.ds(mine * share, share)] = rotated[pl.ds(first_of(mine, me), share)]
    for turn in range(1, parts):
        turn_of(0, turn).start()

    own.wait()
    for step in range(1, bcols):
        gather_of(step, lax.rem(col_id + bcols - step, bcols)).wait_recv()
    for name in ("forward", "smoothing", "inverse"):
        copies[name].wait()
    both = None
    for part in range(bcols):
        term = dot_short(pencils[part], refs["forward"][part])
        both = term if both is None else both + term
    padded = both.shape[1] // 2
    real, imag = both[:, :padded], both[:, padded:]
    weights = lax.rsqrt(dot_short(real * real + imag * imag, refs["smoothing"][...]) + epsilon)
    windows[me, margin : margin + rows] = dot_short(
        real * weights, refs["inverse"][col_id, :padded, :]
    ) + dot_short(imag * weights, refs["inverse"][col_id, padded:, :])

    def window_of(step, plane):
        part = windows.at[plane, pl.ds(margin, rows)]
        return pltpu.make_async_remote_copy(
            src_ref=part,
            dst_ref=part,
            send_sem=send_sems.at[3],
            recv_sem=window_sems.at[step],
            device_id=plane_peer(step),
            device_id_type=MESH,
        )

    def margin_of(step, plane):
        return pltpu.make_async_remote_copy(
            src_ref=windows.at[plane, pl.ds(pl.multiple_of(rows - row_id * (rows - margin), 8), margin)],
            dst_ref=windows.at[plane, pl.ds(pl.multiple_of(row_id * (margin + rows), 8), margin)],
            send_sem=send_sems.at[4 if step == 0 else 3],
            recv_sem=window_sems.at[step],
            device_id=plane_peer(step, 1),
            device_id_type=MESH,
        )

    for step in reversed(range(orients)):
        if step:
            window_of(step, me).start()
        if brows > 1:
            margin_of(step, me).start()
    for name in ("template_lines", "template_rows", "volume_lines", "volume_rows", "score_rows", "score_lines", "box"):
        copies[name].wait()

    def transform(steps):
        tiles = []
        for step in steps:
            plane = partners[step]
            count = (rows if step else 0) + (margin if brows > 1 else 0)
            if count:
                arrived = windows.at[plane, pl.ds(0, count)]
                pltpu.make_async_copy(arrived, arrived, window_sems.at[step]).wait()
            tile = windows[plane, skip : skip + tile_rows]
            gap = plane - me
            near = jnp.logical_and(gap >= -half_edge, gap < half_edge).astype(jnp.float32)
            energy[...] += tile * tile * near
            tiles.append(tile)
        turned = by_table(jnp.concatenate(tiles, axis=0), refs["volume_lines"][...])
        for first in range(0, len(steps), 2):
            pair = []
            for i in range(first, first + 2):
                part = turned[i * tile_rows : (i + 1) * tile_rows]
                pair.append(jnp.concatenate([part[:, :size], part[:, size:]], axis=0))
            spun = table_by(refs["volume_rows"][...], jnp.concatenate(pair, axis=1))
            for i in range(2):
                volumes[partners[steps[first + i]]] = spun[:, i * size : (i + 1) * size]

    def unfold(steps):
        for step in steps:
            if parts > 1:
                arrived = rotations.at[partners[step], pl.ds(0, orients - share)]
                pltpu.make_async_copy(arrived, arrived, turn_sems.at[step]).wait()
        planes = jnp.concatenate([rotations[partners[step]][:, 0, :] for step in steps], axis=0)
        width = span * edge
        pieces = [planes[:, j * width : j * width + LANES] for j in range(strips)]
        turned = by_table(jnp.concatenate(pieces, axis=0), refs["template_lines"][...])
        for k in range(2 * span):
            lines[k] = turned[:, k * size : (k + 1) * size]
        count = len(steps) * orients
        for i, step in enumerate(steps):
            for first in range(0, orients, 2):
                pair = [
                    jnp.concatenate(
                        [lines[k, pl.ds(i * orients + slot, strips, stride=count), :] for k in range(2 * span)],
                        axis=0,
                    )
                    for slot in (first, first + 1)
                ]
                spun = table_by(refs["template_rows"][...], jnp.concatenate(pair, axis=1))
                for j in range(2):
                    templates[partners[step], planes_of[first + j]] = spun[:, j * size : (j + 1) * size]

    def forward(steps):
        for step in steps:
            if step:
                share_of(step, partners[step]).wait_recv()
                for turn in range(1, parts):
                    turn_of(step, turn).start()

    groups = [list(range(first, first + batch)) for first in range(0, orients, batch)]
    for steps in groups:
        forward(steps)
    for steps in groups:
        unfold(steps)
        transform(steps)

    bunch = math.gcd(orients, 8)

    def combine(lowest):
        def gather(held, start):
            held = list(held)
            for i in range(bunch):
                straight = volumes[start + i, :tile_rows, :]
                crossed = volumes[start + i, tile_rows:, :]
                for j in range(2):
                    wave = templates[lowest + j, start + i]
                    held[2 * j] = held[2 * j] + straight * wave
                    held[2 * j + 1] = held[2 * j + 1] + crossed * wave
            return tuple(held)

        held = (jnp.zeros((tile_rows, size), jnp.float32),) * 4
        if orients == bunch:
            held = gather(held, 0)
        else:
            held = lax.fori_loop(0, orients // bunch, lambda i, h: gather(h, i * bunch), held)
        return jnp.concatenate([jnp.concatenate(held[:2], axis=0), jnp.concatenate(held[2:], axis=0)], axis=1)

    def finish(lowest):
        for first in range(0, bunch, 2):
            turned = table_by(refs["score_rows"][...], combine(lowest + first))
            for i in range(2):
                part = turned[:, i * size : (i + 1) * size]
                start = pl.multiple_of((lowest + first + i) * rows, rows)
                scores[pl.ds(start, rows), :size] = part[:rows]
                scores[pl.ds(start, rows), size:] = part[rows:]

    if orients == bunch:
        finish(0)
    else:
        pl.loop(0, orients // bunch)(lambda i: finish(i * bunch))

    summed = energy[0:rows, :]
    for b in range(1, edge):
        summed = summed + energy[b : b + rows, :]
    upper, lower = halves(summed)
    boxed = product(upper, refs["box"][...]) + product(lower, refs["box"][...])
    scaling_ref[0] = lax.rsqrt(boxed / edge**3 + epsilon)
    scored = by_table(scores[...], refs["score_lines"][...])
    best_ref[0] = jnp.max(scored.reshape(orients, rows, cols), axis=0)
    sent = [
        pencils.at[pl.ds(0, bcols - 1)],
        rotations.at[pl.ds(0, orients - 1), pl.ds(0, share)],
        rotations.at[pl.ds(0, orients), pl.ds(0, orients - share)],
        windows.at[pl.ds(0, orients - 1), pl.ds(0, rows + (margin if brows > 1 else 0))],
        windows.at[0, pl.ds(0, margin)],
    ]
    wanted = [bcols > 1, True, parts > 1, True, brows > 1]
    for i, ref in enumerate(sent):
        if wanted[i]:
            pltpu.make_async_copy(ref, ref, send_sems.at[i]).wait()


def dot_short(a, b):
    return jnp.dot(a, b, precision=lax.Precision.HIGH, preferred_element_type=jnp.float32)


names = (
    "template",
    "index",
    "forward",
    "smoothing",
    "inverse",
    "template_lines",
    "template_rows",
    "volume_lines",
    "volume_rows",
    "score_rows",
    "score_lines",
    "box",
)


def staged(sizes, *refs):
    brick, sources = refs[0], refs[1 : len(names) + 1]
    results = refs[len(names) + 1 : len(names) + 3]
    held = refs[len(names) + 3 : 2 * len(names) + 3]
    rest = refs[2 * len(names) + 3 : -1]
    copies = {
        name: pltpu.make_async_copy(source, target, refs[-1].at[i])
        for i, (name, source, target) in enumerate(zip(names, sources, held))
    }
    named = dict(zip(names, held), brick=brick)
    match_kernel(sizes, named, copies, *rest, *results)


def shards(volume, template, voxel_maps):
    orients, brows, bcols = (lax.axis_size(axis) for axis in ("orient", "brow", "bcol"))
    planes, rows, cols = volume.shape
    edge = template.shape[0]
    half_edge = edge // 2
    length = cols * bcols
    size = cols + edge
    tile_rows = rows + edge
    margin = round_up(half_edge, 8)
    strips = 8
    batch = math.gcd(orients, 4)
    parts = brows if orients % (2 * brows) == 0 else 1
    base = half_edge - orients
    assert brows <= 2 and margin <= rows and tile_rows <= rows + 2 * margin
    assert base % 2 == 0 and orients % 2 == 0
    assert edge % strips == 0 and edge // strips * edge <= LANES
    width = edge // strips * edge * (strips - 1) + LANES
    width = round_up(width, LANES)
    vmem = pl.BlockSpec(memory_space=pltpu.VMEM)
    constants = (
        forward_table(length, bcols),
        smoothing_table(length),
        windowed_inverse(length, bcols, half_edge),
        template_lines(edge, size, strips),
        template_rows(tile_rows, edge, strips),
        right_table(line_table(size, size)),
        volume_rows(tile_rows),
        score_rows(tile_rows, rows),
        score_lines(size, cols),
        box_table(size, cols, edge),
    )
    sizes = (orients, brows, bcols, parts, edge, base, margin, batch, strips)
    operands = (volume, template.reshape(edge * edge, edge), voxel_maps)
    operands += tuple(jnp.asarray(c) for c in constants)
    best, scaling = pl.pallas_call(
        lambda *refs: staged(sizes, *refs),
        out_shape=(pltpu.VMEM((1, rows, cols), jnp.float32),) * 2,
        in_specs=[pl.BlockSpec(memory_space=pl.ANY)] * len(operands),
        out_specs=(vmem, vmem),
        scratch_shapes=[pltpu.VMEM(x.shape, x.dtype) for x in operands[1:]]
        + [
            pltpu.VMEM((2 * orients // parts, 1, width), jnp.float32),
            pltpu.VMEM((orients, orients, 1, width), jnp.float32),
            pltpu.VMEM((2 * edge // strips, strips * batch * orients, size), jnp.float32),
            pltpu.VMEM((orients, orients, tile_rows, size), jnp.float32),
            pltpu.VMEM((orients, 2 * tile_rows, size), jnp.float32),
            pltpu.VMEM((bcols, rows, cols), jnp.float32),
            pltpu.VMEM((orients, rows + 2 * margin, size), jnp.float32),
            pltpu.VMEM((tile_rows, size), jnp.float32),
            pltpu.VMEM((orients * rows, 2 * size), jnp.float32),
            pltpu.VMEM((edge * edge, edge), jnp.float32),
            pltpu.SemaphoreType.DMA,
            pltpu.SemaphoreType.DMA((bcols,)),
            pltpu.SemaphoreType.DMA((orients,)),
            pltpu.SemaphoreType.DMA((orients,)),
            pltpu.SemaphoreType.DMA((orients,)),
            pltpu.SemaphoreType.DMA((5,)),
            pltpu.SemaphoreType.DMA((len(names),)),
        ],
        compiler_params=pltpu.CompilerParams(collective_id=0, has_side_effects=True),
        name="match",
    )(*operands)
    return best * scaling


def solution(mesh):
    in_specs = (P("orient", "brow", "bcol"), P(), P("orient", None))
    out_specs = P("orient", "brow", "bcol")
    return jax.shard_map(shards, mesh=mesh, in_specs=in_specs, out_specs=out_specs, check_vma=False)
```

time: 22.6 us -> 18.7 us (0.83)
  Pallas kernels: 21.8 us -> 17.9 us
    pallas_call x1, Pallas kernels: 21.8 us -> 17.9 us  [shards(): pl.pallas_call(lambda *refs: staged(sizes, *refs), out_shape=(pltpu.VMEM(...]
where the time goes in v2:
time: 18.7 us; the launch traced here: 18.5 us
  Pallas kernels  17.9 us (96%)
  other arithmetic  0.61 us (3%)
    pallas_call x1, Pallas kernels, shards(): pl.pallas_call(lambda *refs: staged(sizes, *refs), out_shape=(pltpu.VMEM(...  17.9 us
    mul x1, other arithmetic, shards(): return best * scaling  0.61 us

profile of v2, /device:TPU:0, one launch (start us, length us, event | category | flops | bytes accessed | tf_op | source)
XLA Modules:
  0.0 18.5 jit_solution(9914607563247286743)
XLA Ops:
  0.0 17.9 %match.1 = (f32[1,32,104]{2,1,0:T(8,128)S(1)}, f32[1,32,104]{2,1,0:T(8,128)S(1)}) custom-call(f32[1,32,104]{2,1,0:T(8,128)} %refs_0_.1, f32[576,24]{1,0:T(8,128)} %bitcast.1, s32[1,13824]{1,0:T(1,128)} %refs_2_.1, f32[2,104,256]{2,1,0:T(8,128)} %constant.20.clone.refs_3_, f32[128,128]{1,0:T(8,128)} %constant.21.clone.refs_4_, ...), custom_call_target="tpu_custom_call" | custom-call | tf_op jit(solution)/shard_map/match/pallas_call | solution.py:544
  17.9 0.6 %mul.3 = f32[1,32,104]{2,1,0:T(8,128)} multiply(f32[1,32,104]{2,1,0:T(8,128)S(1)} %get-tuple-element.7, f32[1,32,104]{2,1,0:T(8,128)S(1)} %get-tuple-element.8) | non-fusion elementwise | flops 3328 | bytes 39936 | tf_op jit(solution)/shard_map/mul | solution.py:572

commit v3 on v2

--- a/solution.py
+++ b/solution.py
@@ -185,12 +185,15 @@
     energy,
     scores,
     normed,
+    table,
     own_sem,
     gather_sems,
     share_sems,
     turn_sems,
     window_sems,
+    margin_sems,
     send_sems,
+    tokens,
     best_ref,
     scaling_ref,
 ):
@@ -219,9 +222,19 @@
         return other
 
     partners = [partner(step) for step in range(orients)]
-
-    def plane_peer(step, turn=0):
-        return {"orient": partners[step], "brow": lax.rem(row_id + turn, brows), "bcol": col_id}
+    pair, last = me // 2, orients // 2 - 1
+
+    def plane_peer(plane):
+        return {"orient": plane, "brow": row_id, "bcol": col_id}
+
+    def row_peer(turn):
+        return {"orient": me, "brow": lax.rem(row_id + turn, brows), "bcol": col_id}
+
+    def target(k):
+        return k + (k + orients - me) // orients
+
+    def greet(semaphore, peer):
+        pl.semaphore_signal(semaphore, inc=1, device_id=peer, device_id_type=MESH)
 
     def first_of(part, plane):
         start = orients - plane
@@ -236,11 +249,21 @@
     windows[...] = jnp.zeros_like(windows)
     barrier = pltpu.get_barrier_semaphore()
     for step in range(1, bcols):
-        pl.semaphore_signal(barrier, inc=1, device_id=column_peer(step), device_id_type=MESH)
-    for step in range(orients):
-        for turn in range(brows):
-            if step or turn:
-                pl.semaphore_signal(barrier, inc=1, device_id=plane_peer(step, turn), device_id_type=MESH)
+        greet(barrier, column_peer(step))
+    for turn in range(1, brows):
+        greet(barrier, row_peer(turn))
+    greet(barrier, plane_peer(partners[1]))
+
+    @pl.when(pair > 0)
+    def _():
+        for i in range(2):
+            greet(barrier, plane_peer(2 * pair - 2 + i))
+
+    @pl.when(pair < last)
+    def _():
+        for i in range(2):
+            greet(barrier, plane_peer(2 * pair + 2 + i))
+
     for copy in copies.values():
         copy.start()
     own = pltpu.make_async_copy(refs["brick"].at[0], pencils.at[col_id], own_sem)
@@ -248,7 +271,35 @@
     energy[...] = jnp.zeros_like(energy)
     rotated[...] = jnp.zeros_like(rotated)
     planes_of = [plane_of(slot) for slot in range(orients)]
-    pl.semaphore_wait(barrier, bcols - 1 + orients * brows - 1)
+
+    def tabulate():
+        copies["template"].wait()
+        table[...] = split_table(refs["template"], normed)
+        copies["index"].wait()
+
+    def find(first, end):
+        @pl.loop(first, end)
+        def _(index):
+            plane = base + 2 * mine + 2 * parts * index
+
+            def fill():
+                start = pl.multiple_of(plane * plane_voxels, 2 * plane_voxels)
+                found = look_up(table[...], refs["index"][0:1, pl.ds(start, 2 * plane_voxels)])
+                for i in range(2):
+                    rotated[2 * index + i, :, :plane_voxels] = found[:, i * plane_voxels : (i + 1) * plane_voxels]
+
+            if base < 0 or base + 2 * orients > edge:
+                pl.when(jnp.logical_and(plane >= 0, plane < edge))(fill)
+            else:
+                fill()
+
+    @pl.when(pair < last)
+    def _():
+        tabulate()
+        find(0, share // 2)
+
+    beside = (pair + last) // (last + 1) + (2 * last - pair) // (last + 1)
+    pl.semaphore_wait(barrier, bcols - 1 + brows - 1 + 1 + 2 * beside)
 
     def gather_of(step, place):
         return pltpu.make_async_remote_copy(
@@ -263,53 +314,100 @@
     for step in range(1, bcols):
         gather_of(step, col_id).start()
 
-    copies["template"].wait()
-    pieces = split_table(refs["template"], normed)
-    copies["index"].wait()
-
-    @pl.loop(0, orients // parts)
-    def _(pair):
-        plane = base + 2 * mine + 2 * parts * pair
-
-        def fill():
-            start = pl.multiple_of(plane * plane_voxels, 2 * plane_voxels)
-            found = look_up(pieces, refs["index"][0:1, pl.ds(start, 2 * plane_voxels)])
-            for i in range(2):
-                rotated[2 * pair + i, :, :plane_voxels] = found[:, i * plane_voxels : (i + 1) * plane_voxels]
-
-        if base < 0 or base + 2 * orients > edge:
-            pl.when(jnp.logical_and(plane >= 0, plane < edge))(fill)
-        else:
-            fill()
+    lower, upper = tokens.at[0], tokens.at[1]
+    above, below = plane_peer(me + 2), plane_peer(me - 2)
+
+    @pl.when(jnp.logical_and(pair == last - 1, pair > 0))
+    def _():
+        greet(upper, below)
+
+    @pl.when(jnp.logical_and(pair == 1, pair < last))
+    def _():
+        greet(lower, above)
+
+    @pl.when(jnp.logical_and(pair > 1, pair < last))
+    def _():
+        pl.semaphore_wait(lower, 1)
+        greet(lower, above)
+
+    @pl.when(pair == last)
+    def _():
+        tabulate()
+        find(0, share // 2)
+
+    find(share // 2, share)
 
     def block(rotation, part):
         return rotations.at[rotation, pl.ds(part * share, share)]
 
-    def share_of(step, rotation):
+    def share_of(plane):
         return pltpu.make_async_remote_copy(
-            src_ref=rotated.at[pl.ds(first_of(mine, partners[step]), share)],
-            dst_ref=block(rotation, mine),
+            src_ref=rotated.at[pl.ds(first_of(mine, plane), share)],
+            dst_ref=block(me, mine),
             send_sem=send_sems.at[1],
-            recv_sem=share_sems.at[step],
-            device_id=plane_peer(step),
+            recv_sem=share_sems.at[me],
+            device_id=plane_peer(plane),
             device_id_type=MESH,
         )
 
-    def turn_of(step, turn):
+    def turn_of(rotation, turn):
         return pltpu.make_async_remote_copy(
-            src_ref=block(partners[step], mine),
-            dst_ref=block(partners[step], mine),
+            src_ref=block(rotation, mine),
+            dst_ref=block(rotation, mine),
             send_sem=send_sems.at[2],
-            recv_sem=turn_sems.at[step],
-            device_id=plane_peer(0, turn),
+            recv_sem=turn_sems.at[rotation],
+            device_id=row_peer(turn),
             device_id_type=MESH,
         )
 
-    for step in reversed(range(1, orients)):
-        share_of(step, me).start()
     rotations[me, pl.ds(mine * share, share)] = rotated[pl.ds(first_of(mine, me), share)]
     for turn in range(1, parts):
-        turn_of(0, turn).start()
+        turn_of(me, turn).start()
+    share_of(partners[1]).start()
+
+    @pl.when(pair > 0)
+    def _():
+        for i in range(2):
+            share_of(2 * pair - 2 + i).start()
+
+    @pl.when(pair < last)
+    def _():
+        for i in range(2):
+            share_of(2 * pair + 2 + i).start()
+
+    @pl.when(pair < last - 1)
+    def _():
+        pl.semaphore_wait(upper, 1)
+
+    @pl.when(jnp.logical_and(pair > 0, pair < last - 1))
+    def _():
+        greet(upper, below)
+
+    @pl.when(jnp.logical_and(pair > 1, pair == last))
+    def _():
+        pl.semaphore_wait(lower, 1)
+
+    for other in range(last + 1):
+
+        @pl.when(jnp.logical_or(other > pair + 1, other < pair - 1))
+        def _():
+            for i in range(2):
+                share_of(2 * other + i).start()
+
+    def forward(steps):
+        for step in steps:
+            if step:
+                arrived = block(partners[step], mine)
+                pltpu.make_async_copy(arrived, arrived, share_sems.at[partners[step]]).wait()
+                for turn in range(1, parts):
+                    turn_of(partners[step], turn).start()
+
+    groups = [list(range(first, first + batch)) for first in range(0, orients, batch)]
+    early = 2 * pair < last
+
+    @pl.when(early)
+    def _():
+        forward(groups[0])
 
     own.wait()
     for step in range(1, bcols):
@@ -327,32 +425,31 @@
         real * weights, refs["inverse"][col_id, :padded, :]
     ) + dot_short(imag * weights, refs["inverse"][col_id, padded:, :])
 
-    def window_of(step, plane):
-        part = windows.at[plane, pl.ds(margin, rows)]
+    def window_of(plane):
+        part = windows.at[me, pl.ds(margin, rows)]
         return pltpu.make_async_remote_copy(
             src_ref=part,
             dst_ref=part,
             send_sem=send_sems.at[3],
-            recv_sem=window_sems.at[step],
-            device_id=plane_peer(step),
+            recv_sem=window_sems.at[me],
+            device_id=plane_peer(plane),
             device_id_type=MESH,
         )
 
-    def margin_of(step, plane):
+    def margin_of(plane):
         return pltpu.make_async_remote_copy(
             src_ref=windows.at[plane, pl.ds(pl.multiple_of(rows - row_id * (rows - margin), 8), margin)],
             dst_ref=windows.at[plane, pl.ds(pl.multiple_of(row_id * (margin + rows), 8), margin)],
-            send_sem=send_sems.at[4 if step == 0 else 3],
-            recv_sem=window_sems.at[step],
-            device_id=plane_peer(step, 1),
+            send_sem=send_sems.at[4],
+            recv_sem=margin_sems.at[plane],
+            device_id=row_peer(1),
             device_id_type=MESH,
         )
 
-    for step in reversed(range(orients)):
-        if step:
-            window_of(step, me).start()
-        if brows > 1:
-            margin_of(step, me).start()
+    for k in range(orients - 1):
+        window_of(target(k)).start()
+    if brows > 1:
+        margin_of(me).start()
     for name in ("template_lines", "template_rows", "volume_lines", "volume_rows", "score_rows", "score_lines", "box"):
         copies[name].wait()
 
@@ -360,10 +457,9 @@
         tiles = []
         for step in steps:
             plane = partners[step]
-            count = (rows if step else 0) + (margin if brows > 1 else 0)
-            if count:
-                arrived = windows.at[plane, pl.ds(0, count)]
-                pltpu.make_async_copy(arrived, arrived, window_sems.at[step]).wait()
+            if brows > 1:
+                arrived = windows.at[plane, pl.ds(0, margin)]
+                pltpu.make_async_copy(arrived, arrived, margin_sems.at[plane]).wait()
             tile = windows[plane, skip : skip + tile_rows]
             gap = plane - me
             near = jnp.logical_and(gap >= -half_edge, gap < half_edge).astype(jnp.float32)
@@ -383,7 +479,7 @@
         for step in steps:
             if parts > 1:
                 arrived = rotations.at[partners[step], pl.ds(0, orients - share)]
-                pltpu.make_async_copy(arrived, arrived, turn_sems.at[step]).wait()
+                pltpu.make_async_copy(arrived, arrived, turn_sems.at[partners[step]]).wait()
         planes = jnp.concatenate([rotations[partners[step]][:, 0, :] for step in steps], axis=0)
         width = span * edge
         pieces = [planes[:, j * width : j * width + LANES] for j in range(strips)]
@@ -404,18 +500,26 @@
                 for j in range(2):
                     templates[partners[step], planes_of[first + j]] = spun[:, j * size : (j + 1) * size]
 
-    def forward(steps):
+    def spread(steps):
         for step in steps:
             if step:
-                share_of(step, partners[step]).wait_recv()
-                for turn in range(1, parts):
-                    turn_of(step, turn).start()
-
-    groups = [list(range(first, first + batch)) for first in range(0, orients, batch)]
-    for steps in groups:
+                arrived = windows.at[partners[step], pl.ds(margin, rows)]
+                pltpu.make_async_copy(arrived, arrived, window_sems.at[partners[step]]).wait()
+                if brows > 1:
+                    margin_of(partners[step]).start()
+
+    @pl.when(jnp.logical_not(early))
+    def _():
+        forward(groups[0])
+
+    unfold(groups[0])
+    for steps in groups[1:]:
         forward(steps)
     for steps in groups:
+        spread(steps)
+    for steps in groups[1:]:
         unfold(steps)
+    for steps in groups:
         transform(steps)
 
     bunch = math.gcd(orients, 8)
@@ -465,8 +569,8 @@
         pencils.at[pl.ds(0, bcols - 1)],
         rotations.at[pl.ds(0, orients - 1), pl.ds(0, share)],
         rotations.at[pl.ds(0, orients), pl.ds(0, orients - share)],
-        windows.at[pl.ds(0, orients - 1), pl.ds(0, rows + (margin if brows > 1 else 0))],
-        windows.at[0, pl.ds(0, margin)],
+        windows.at[pl.ds(0, orients - 1), pl.ds(margin, rows)],
+        windows.at[pl.ds(0, orients), pl.ds(0, margin)],
     ]
     wanted = [bcols > 1, True, parts > 1, True, brows > 1]
     for i, ref in enumerate(sent):
@@ -558,12 +662,15 @@
             pltpu.VMEM((tile_rows, size), jnp.float32),
             pltpu.VMEM((orients * rows, 2 * size), jnp.float32),
             pltpu.VMEM((edge * edge, edge), jnp.float32),
+            pltpu.VMEM((2 * round_up(edge * edge // 8, 16), 8 * edge), jnp.bfloat16),
             pltpu.SemaphoreType.DMA,
             pltpu.SemaphoreType.DMA((bcols,)),
             pltpu.SemaphoreType.DMA((orients,)),
             pltpu.SemaphoreType.DMA((orients,)),
             pltpu.SemaphoreType.DMA((orients,)),
+            pltpu.SemaphoreType.DMA((orients,)),
             pltpu.SemaphoreType.DMA((5,)),
+            pltpu.SemaphoreType.REGULAR((2,)),
             pltpu.SemaphoreType.DMA((len(names),)),
         ],
         compiler_params=pltpu.CompilerParams(collective_id=0, has_side_effects=True),

time: 18.7 us -> 17.5 us (0.936)
  Pallas kernels: 17.9 us -> 16.8 us
    pallas_call x1, Pallas kernels: 17.9 us -> 16.8 us  [shards(): pl.pallas_call(lambda *refs: staged(sizes, *refs), out_shape=(pltpu.VMEM(...]
where the time goes in v3:
time: 17.5 us; the launch traced here: 17.4 us
  Pallas kernels  16.8 us (96%)
  other arithmetic  0.61 us (3%)
    pallas_call x1, Pallas kernels, shards(): pl.pallas_call(lambda *refs: staged(sizes, *refs), out_shape=(pltpu.VMEM(...  16.8 us
    mul x1, other arithmetic, shards(): return best * scaling  0.61 us

profile of v3, /device:TPU:0, one launch (start us, length us, event | category | flops | bytes accessed | tf_op | source)
XLA Modules:
  0.0 17.4 jit_solution(13548003375686840805)
XLA Ops:
  0.0 16.8 %match.1 = (f32[1,32,104]{2,1,0:T(8,128)S(1)}, f32[1,32,104]{2,1,0:T(8,128)S(1)}) custom-call(f32[1,32,104]{2,1,0:T(8,128)} %refs_0_.1, f32[576,24]{1,0:T(8,128)} %bitcast.1, s32[1,13824]{1,0:T(1,128)} %refs_2_.1, f32[2,104,256]{2,1,0:T(8,128)} %constant.20.clone.refs_3_, f32[128,128]{1,0:T(8,128)} %constant.21.clone.refs_4_, ...), custom_call_target="tpu_custom_call" | custom-call | tf_op jit(solution)/shard_map/match/pallas_call | solution.py:648
  16.8 0.6 %mul.3 = f32[1,32,104]{2,1,0:T(8,128)} multiply(f32[1,32,104]{2,1,0:T(8,128)S(1)} %get-tuple-element.7, f32[1,32,104]{2,1,0:T(8,128)S(1)} %get-tuple-element.8) | non-fusion elementwise | flops 3328 | bytes 39936 | tf_op jit(solution)/shard_map/mul | solution.py:679

commit v4 on v3

--- a/solution.py
+++ b/solution.py
@@ -210,8 +210,8 @@
     plane_voxels = edge * edge
     span = edge // strips
 
-    def column_peer(step):
-        return {"orient": me, "brow": row_id, "bcol": lax.rem(col_id + step, bcols)}
+    def column_peer(column):
+        return {"orient": me, "brow": row_id, "bcol": column}
 
     def partner(step):
         assert orients & (orients - 1) == 0
@@ -223,15 +223,24 @@
 
     partners = [partner(step) for step in range(orients)]
     pair, last = me // 2, orients // 2 - 1
+    odd = lax.rem(me, 2)
+    by_column, by_row, by_pair, by_near, by_far = (tokens.at[i] for i in range(5))
 
     def plane_peer(plane):
         return {"orient": plane, "brow": row_id, "bcol": col_id}
 
-    def row_peer(turn):
-        return {"orient": me, "brow": lax.rem(row_id + turn, brows), "bcol": col_id}
-
-    def target(k):
-        return k + (k + orients - me) // orients
+    def row_peer(row):
+        return {"orient": me, "brow": row, "bcol": col_id}
+
+    def expect(semaphore, count):
+        pl.when(count > 0)(lambda: pl.semaphore_wait(semaphore, count))
+
+    def each(count, own, step, do):
+        for other in range(count):
+
+            @pl.when(step * other > step * own)
+            def _():
+                do(other)
 
     def greet(semaphore, peer):
         pl.semaphore_signal(semaphore, inc=1, device_id=peer, device_id_type=MESH)
@@ -248,22 +257,16 @@
 
     windows[...] = jnp.zeros_like(windows)
     barrier = pltpu.get_barrier_semaphore()
-    for step in range(1, bcols):
-        greet(barrier, column_peer(step))
-    for turn in range(1, brows):
-        greet(barrier, row_peer(turn))
-    greet(barrier, plane_peer(partners[1]))
-
-    @pl.when(pair > 0)
+    @pl.when(odd == 0)
     def _():
-        for i in range(2):
-            greet(barrier, plane_peer(2 * pair - 2 + i))
-
-    @pl.when(pair < last)
+        each(orients, me, 1, lambda plane: greet(barrier, plane_peer(plane)))
+
+    @pl.when(odd == 1)
     def _():
-        for i in range(2):
-            greet(barrier, plane_peer(2 * pair + 2 + i))
-
+        each(orients // 2, pair, 1, lambda other: greet(barrier, plane_peer(2 * other + 1)))
+
+    each(bcols, col_id, 1, lambda column: greet(barrier, column_peer(column)))
+    each(brows, row_id, 1, lambda row: greet(barrier, row_peer(row)))
     for copy in copies.values():
         copy.start()
     own = pltpu.make_async_copy(refs["brick"].at[0], pencils.at[col_id], own_sem)
@@ -293,49 +296,42 @@
             else:
                 fill()
 
-    @pl.when(pair < last)
-    def _():
-        tabulate()
-        find(0, share // 2)
-
-    beside = (pair + last) // (last + 1) + (2 * last - pair) // (last + 1)
-    pl.semaphore_wait(barrier, bcols - 1 + brows - 1 + 1 + 2 * beside)
-
-    def gather_of(step, place):
+    expect(barrier, pair + odd * (pair + 1) + col_id + row_id)
+
+    def gather_of(column):
         return pltpu.make_async_remote_copy(
             src_ref=refs["brick"].at[0],
-            dst_ref=pencils.at[place],
+            dst_ref=pencils.at[col_id],
             send_sem=send_sems.at[0],
-            recv_sem=gather_sems.at[step],
-            device_id=column_peer(step),
+            recv_sem=gather_sems.at[col_id],
+            device_id=column_peer(column),
             device_id_type=MESH,
         )
 
-    for step in range(1, bcols):
-        gather_of(step, col_id).start()
-
-    lower, upper = tokens.at[0], tokens.at[1]
-    above, below = plane_peer(me + 2), plane_peer(me - 2)
-
-    @pl.when(jnp.logical_and(pair == last - 1, pair > 0))
+    each(bcols, col_id, -1, lambda column: gather_of(column).start())
+    each(bcols, col_id, -1, lambda column: greet(by_column, column_peer(column)))
+    each(brows, row_id, -1, lambda row: greet(by_row, row_peer(row)))
+
+    @pl.when(odd == 1)
     def _():
-        greet(upper, below)
-
-    @pl.when(jnp.logical_and(pair == 1, pair < last))
-    def _():
-        greet(lower, above)
-
-    @pl.when(jnp.logical_and(pair > 1, pair < last))
-    def _():
-        pl.semaphore_wait(lower, 1)
-        greet(lower, above)
-
-    @pl.when(pair == last)
-    def _():
-        tabulate()
-        find(0, share // 2)
-
-    find(share // 2, share)
+        def answer(other):
+            for i in range(2):
+                greet(by_far, plane_peer(2 * other + i))
+
+        greet(by_pair, plane_peer(me - 1))
+        each(orients // 2, pair - 1, -1, answer)
+
+        @pl.when(pair > 0)
+        def _():
+            for i in range(2):
+                greet(by_near, plane_peer(2 * pair - 2 + i))
+
+    tabulate()
+    find(0, share // 4)
+    expect(by_column, bcols - 1 - col_id)
+    each(bcols, col_id, 1, lambda column: gather_of(column).start())
+    find(share // 4, share)
+    expect(by_row, brows - 1 - row_id)
 
     def block(rotation, part):
         return rotations.at[rotation, pl.ds(part * share, share)]
@@ -351,48 +347,36 @@
         )
 
     def turn_of(rotation, turn):
+        row = lax.rem(row_id + turn, brows)
         return pltpu.make_async_remote_copy(
             src_ref=block(rotation, mine),
             dst_ref=block(rotation, mine),
             send_sem=send_sems.at[2],
             recv_sem=turn_sems.at[rotation],
-            device_id=row_peer(turn),
+            device_id=row_peer(row),
             device_id_type=MESH,
         )
 
     rotations[me, pl.ds(mine * share, share)] = rotated[pl.ds(first_of(mine, me), share)]
     for turn in range(1, parts):
         turn_of(me, turn).start()
-    share_of(partners[1]).start()
-
-    @pl.when(pair > 0)
-    def _():
-        for i in range(2):
-            share_of(2 * pair - 2 + i).start()
-
-    @pl.when(pair < last)
-    def _():
-        for i in range(2):
-            share_of(2 * pair + 2 + i).start()
-
-    @pl.when(pair < last - 1)
-    def _():
-        pl.semaphore_wait(upper, 1)
-
-    @pl.when(jnp.logical_and(pair > 0, pair < last - 1))
-    def _():
-        greet(upper, below)
-
-    @pl.when(jnp.logical_and(pair > 1, pair == last))
-    def _():
-        pl.semaphore_wait(lower, 1)
-
-    for other in range(last + 1):
-
-        @pl.when(jnp.logical_or(other > pair + 1, other < pair - 1))
-        def _():
-            for i in range(2):
-                share_of(2 * other + i).start()
+    expect(by_pair, 1 - odd)
+    each(orients, me, -1, lambda plane: share_of(plane).start())
+    pl.when(odd == 0)(lambda: share_of(me + 1).start())
+    near = (2 * last - pair) // (last + 1)
+    far = last - pair - near
+
+    def send(kind, planes):
+        def one(plane):
+            if planes == "near":
+                pl.when(plane < 2 * pair + 4)(lambda: kind(plane).start())
+            else:
+                pl.when(plane >= 2 * pair + 4)(lambda: kind(plane).start())
+
+        each(orients, 2 * pair + 1, 1, one)
+
+    expect(by_near, near)
+    send(share_of, "near")
 
     def forward(steps):
         for step in steps:
@@ -403,15 +387,11 @@
                     turn_of(partners[step], turn).start()
 
     groups = [list(range(first, first + batch)) for first in range(0, orients, batch)]
-    early = 2 * pair < last
-
-    @pl.when(early)
-    def _():
-        forward(groups[0])
-
     own.wait()
     for step in range(1, bcols):
-        gather_of(step, lax.rem(col_id + bcols - step, bcols)).wait_recv()
+        column = lax.rem(col_id + step, bcols)
+        arrived = pencils.at[column]
+        pltpu.make_async_copy(arrived, arrived, gather_sems.at[column]).wait()
     for name in ("forward", "smoothing", "inverse"):
         copies[name].wait()
     both = None
@@ -442,12 +422,13 @@
             dst_ref=windows.at[plane, pl.ds(pl.multiple_of(row_id * (margin + rows), 8), margin)],
             send_sem=send_sems.at[4],
             recv_sem=margin_sems.at[plane],
-            device_id=row_peer(1),
+            device_id=row_peer(lax.rem(row_id + 1, brows)),
             device_id_type=MESH,
         )
 
-    for k in range(orients - 1):
-        window_of(target(k)).start()
+    each(orients, me, -1, lambda plane: window_of(plane).start())
+    pl.when(odd == 0)(lambda: window_of(me + 1).start())
+    send(window_of, "near")
     if brows > 1:
         margin_of(me).start()
     for name in ("template_lines", "template_rows", "volume_lines", "volume_rows", "score_rows", "score_lines", "box"):
@@ -480,18 +461,19 @@
             if parts > 1:
                 arrived = rotations.at[partners[step], pl.ds(0, orients - share)]
                 pltpu.make_async_copy(arrived, arrived, turn_sems.at[partners[step]]).wait()
-        planes = jnp.concatenate([rotations[partners[step]][:, 0, :] for step in steps], axis=0)
         width = span * edge
-        pieces = [planes[:, j * width : j * width + LANES] for j in range(strips)]
+        pieces = []
+        for step in steps:
+            planes = rotations[partners[step]][:, 0, :]
+            pieces += [planes[:, j * width : j * width + LANES] for j in range(strips)]
         turned = by_table(jnp.concatenate(pieces, axis=0), refs["template_lines"][...])
         for k in range(2 * span):
             lines[k] = turned[:, k * size : (k + 1) * size]
-        count = len(steps) * orients
         for i, step in enumerate(steps):
             for first in range(0, orients, 2):
                 pair = [
                     jnp.concatenate(
-                        [lines[k, pl.ds(i * orients + slot, strips, stride=count), :] for k in range(2 * span)],
+                        [lines[k, pl.ds(i * strips * orients + slot, strips, stride=orients), :] for k in range(2 * span)],
                         axis=0,
                     )
                     for slot in (first, first + 1)
@@ -508,18 +490,18 @@
                 if brows > 1:
                     margin_of(partners[step]).start()
 
-    @pl.when(jnp.logical_not(early))
-    def _():
-        forward(groups[0])
-
+    forward(groups[0])
+    expect(by_far, far)
+    send(share_of, "far")
+    send(window_of, "far")
     unfold(groups[0])
+    spread(groups[0])
     for steps in groups[1:]:
         forward(steps)
-    for steps in groups:
-        spread(steps)
+    transform(groups[0])
     for steps in groups[1:]:
         unfold(steps)
-    for steps in groups:
+        spread(steps)
         transform(steps)
 
     bunch = math.gcd(orients, 8)
@@ -670,7 +652,7 @@
             pltpu.SemaphoreType.DMA((orients,)),
             pltpu.SemaphoreType.DMA((orients,)),
             pltpu.SemaphoreType.DMA((5,)),
-            pltpu.SemaphoreType.REGULAR((2,)),
+            pltpu.SemaphoreType.REGULAR((5,)),
             pltpu.SemaphoreType.DMA((len(names),)),
         ],
         compiler_params=pltpu.CompilerParams(collective_id=0, has_side_effects=True),

time: 17.5 us -> 16.4 us (0.937)
  Pallas kernels: 16.8 us -> 15.5 us
    pallas_call x1, Pallas kernels: 16.8 us -> 15.5 us  [shards(): pl.pallas_call(lambda *refs: staged(sizes, *refs), out_shape=(pltpu.VMEM(...]
where the time goes in v4:
time: 16.4 us; the launch traced here: 16.1 us
  Pallas kernels  15.5 us (95%)
  other arithmetic  0.61 us (4%)
    pallas_call x1, Pallas kernels, shards(): pl.pallas_call(lambda *refs: staged(sizes, *refs), out_shape=(pltpu.VMEM(...  15.5 us
    mul x1, other arithmetic, shards(): return best * scaling  0.61 us

profile of v4, /device:TPU:0, one launch (start us, length us, event | category | flops | bytes accessed | tf_op | source)
XLA Modules:
  0.0 16.1 jit_solution(8911751172920519765)
XLA Ops:
  0.0 15.5 %match.1 = (f32[1,32,104]{2,1,0:T(8,128)S(1)}, f32[1,32,104]{2,1,0:T(8,128)S(1)}) custom-call(f32[1,32,104]{2,1,0:T(8,128)} %refs_0_.1, f32[576,24]{1,0:T(8,128)} %bitcast.1, s32[1,13824]{1,0:T(1,128)} %refs_2_.1, f32[2,104,256]{2,1,0:T(8,128)} %constant.20.clone.refs_3_, f32[128,128]{1,0:T(8,128)} %constant.21.clone.refs_4_, ...), custom_call_target="tpu_custom_call" | custom-call | tf_op jit(solution)/shard_map/match/pallas_call | solution.py:630
  15.5 0.6 %mul.3 = f32[1,32,104]{2,1,0:T(8,128)} multiply(f32[1,32,104]{2,1,0:T(8,128)S(1)} %get-tuple-element.7, f32[1,32,104]{2,1,0:T(8,128)S(1)} %get-tuple-element.8) | non-fusion elementwise | flops 3328 | bytes 39936 | tf_op jit(solution)/shard_map/mul | solution.py:661

commit v5 on v4

--- a/solution.py
+++ b/solution.py
@@ -123,30 +123,27 @@
     return ((offsets >= 0) & (offsets < edge)).astype(jnp.bfloat16)
 
 
-def split_table(template_ref, normed):
+def split_table(template_ref, shifted):
     lines, edge = template_ref.shape
-    template = template_ref[...]
-    centred = template - jnp.sum(template, keepdims=True) / (lines * edge)
-    normed[...] = centred / jnp.sqrt(jnp.sum(centred * centred, keepdims=True) + epsilon)
-    table = jnp.concatenate([normed[pl.ds(j, lines // 8, stride=8), :] for j in range(8)], axis=1)
+    template = template_ref[...] - 0.5
+    shifted[...] = template
+    mean = jnp.sum(template, keepdims=True) / (lines * edge)
+    centred = template - mean
+    scale = lax.rsqrt(jnp.sum(centred * centred, keepdims=True) + epsilon)
+    table = jnp.concatenate([shifted[pl.ds(j, lines // 8, stride=8), :] for j in range(8)], axis=1)
     spare = round_up(lines // 8, 16) - lines // 8
     table = jnp.concatenate([table, jnp.zeros((spare, 8 * edge), jnp.float32)], axis=0)
-    upper = table.astype(jnp.bfloat16)
-    lower = (table - upper.astype(jnp.float32)).astype(jnp.bfloat16)
-    return jnp.concatenate([upper, lower], axis=0)
+    return jnp.concatenate(halves(table), axis=0), mean, scale
 
 
 def look_up(pieces, index):
     count, span = pieces.shape
     width = index.shape[1]
     high = ((index.astype(jnp.float32) + 0.5) * (1.0 / span)).astype(jnp.int32)
-    low = index - high * span
-    chosen = lax.broadcasted_iota(jnp.int32, (span, width), 0) == low
-    lanes = jnp.dot(
-        pieces,
-        jnp.where(chosen, 1.0, 0.0).astype(jnp.bfloat16),
-        preferred_element_type=jnp.float32,
-    )
+    low = (index - high * span).astype(jnp.float32).astype(jnp.bfloat16)
+    row = lax.broadcasted_iota(jnp.int32, (span, width), 0).astype(jnp.float32).astype(jnp.bfloat16)
+    one = jnp.ones((), jnp.bfloat16)
+    lanes = product(pieces, jnp.where(row == low, one, jnp.zeros_like(one)))
     lanes = lanes[: count // 2] + lanes[count // 2 :]
     mine = lax.broadcasted_iota(jnp.int32, lanes.shape, 0) == high
     return jnp.sum(jnp.where(mine, lanes, 0.0), axis=0, keepdims=True)
@@ -186,6 +183,7 @@
     scores,
     normed,
     table,
+    stats,
     own_sem,
     gather_sems,
     share_sems,
@@ -267,8 +265,10 @@
 
     each(bcols, col_id, 1, lambda column: greet(barrier, column_peer(column)))
     each(brows, row_id, 1, lambda row: greet(barrier, row_peer(row)))
-    for copy in copies.values():
-        copy.start()
+    tables = ("template_lines", "template_rows", "volume_lines", "volume_rows", "score_rows", "score_lines", "box")
+    for name, copy in copies.items():
+        if name not in tables:
+            copy.start()
     own = pltpu.make_async_copy(refs["brick"].at[0], pencils.at[col_id], own_sem)
     own.start()
     energy[...] = jnp.zeros_like(energy)
@@ -277,17 +277,17 @@
 
     def tabulate():
         copies["template"].wait()
-        table[...] = split_table(refs["template"], normed)
+        table[...], stats[0:1, 0:1], stats[1:2, 0:1] = split_table(refs["template"], normed)
         copies["index"].wait()
 
     def find(first, end):
-        @pl.loop(first, end)
-        def _(index):
+        def one(index):
             plane = base + 2 * mine + 2 * parts * index
 
             def fill():
                 start = pl.multiple_of(plane * plane_voxels, 2 * plane_voxels)
                 found = look_up(table[...], refs["index"][0:1, pl.ds(start, 2 * plane_voxels)])
+                found = (found - stats[0:1, 0:1]) * stats[1:2, 0:1]
                 for i in range(2):
                     rotated[2 * index + i, :, :plane_voxels] = found[:, i * plane_voxels : (i + 1) * plane_voxels]
 
@@ -295,6 +295,12 @@
                 pl.when(jnp.logical_and(plane >= 0, plane < edge))(fill)
             else:
                 fill()
+
+        if share <= 4:
+            for index in range(first, end):
+                one(index)
+        else:
+            pl.loop(first, end)(one)
 
     expect(barrier, pair + odd * (pair + 1) + col_id + row_id)
 
@@ -326,11 +332,13 @@
             for i in range(2):
                 greet(by_near, plane_peer(2 * pair - 2 + i))
 
+    for name in tables:
+        copies[name].start()
     tabulate()
-    find(0, share // 4)
+    find(0, share // 2)
     expect(by_column, bcols - 1 - col_id)
     each(bcols, col_id, 1, lambda column: gather_of(column).start())
-    find(share // 4, share)
+    find(share // 2, share)
     expect(by_row, brows - 1 - row_id)
 
     def block(rotation, part):
@@ -431,7 +439,7 @@
     send(window_of, "near")
     if brows > 1:
         margin_of(me).start()
-    for name in ("template_lines", "template_rows", "volume_lines", "volume_rows", "score_rows", "score_lines", "box"):
+    for name in tables:
         copies[name].wait()
 
     def transform(steps):
@@ -645,6 +653,7 @@
             pltpu.VMEM((orients * rows, 2 * size), jnp.float32),
             pltpu.VMEM((edge * edge, edge), jnp.float32),
             pltpu.VMEM((2 * round_up(edge * edge // 8, 16), 8 * edge), jnp.bfloat16),
+            pltpu.VMEM((8, LANES), jnp.float32),
             pltpu.SemaphoreType.DMA,
             pltpu.SemaphoreType.DMA((bcols,)),
             pltpu.SemaphoreType.DMA((orients,)),

time: 16.4 us -> 16.3 us (level)
  no operation moved by 1% of the time
where the time goes in v5:
time: 16.3 us; the launch traced here: 16.2 us
  Pallas kernels  15.6 us (96%)
  other arithmetic  0.61 us (4%)
    pallas_call x1, Pallas kernels, shards(): pl.pallas_call(lambda *refs: staged(sizes, *refs), out_shape=(pltpu.VMEM(...  15.6 us
    mul x1, other arithmetic, shards(): return best * scaling  0.61 us

profile of v5, /device:TPU:0, one launch (start us, length us, event | category | flops | bytes accessed | tf_op | source)
XLA Modules:
  0.0 16.2 jit_solution(8917088175491148432)
XLA Ops:
  0.0 15.6 %match.1 = (f32[1,32,104]{2,1,0:T(8,128)S(1)}, f32[1,32,104]{2,1,0:T(8,128)S(1)}) custom-call(f32[1,32,104]{2,1,0:T(8,128)} %refs_0_.1, f32[576,24]{1,0:T(8,128)} %bitcast.1, s32[1,13824]{1,0:T(1,128)} %refs_2_.1, f32[2,104,256]{2,1,0:T(8,128)} %constant.20.clone.refs_3_, f32[128,128]{1,0:T(8,128)} %constant.21.clone.refs_4_, ...), custom_call_target="tpu_custom_call" | custom-call | tf_op jit(solution)/shard_map/match/pallas_call | solution.py:638
  15.6 0.6 %mul.3 = f32[1,32,104]{2,1,0:T(8,128)} multiply(f32[1,32,104]{2,1,0:T(8,128)S(1)} %get-tuple-element.7, f32[1,32,104]{2,1,0:T(8,128)S(1)} %get-tuple-element.8) | non-fusion elementwise | flops 3328 | bytes 39936 | tf_op jit(solution)/shard_map/mul | solution.py:670

commit v6 on v5

--- a/solution.py
+++ b/solution.py
@@ -304,9 +304,9 @@
 
     expect(barrier, pair + odd * (pair + 1) + col_id + row_id)
 
-    def gather_of(column):
+    def gather_of(column, brick):
         return pltpu.make_async_remote_copy(
-            src_ref=refs["brick"].at[0],
+            src_ref=brick,
             dst_ref=pencils.at[col_id],
             send_sem=send_sems.at[0],
             recv_sem=gather_sems.at[col_id],
@@ -314,7 +314,7 @@
             device_id_type=MESH,
         )
 
-    each(bcols, col_id, -1, lambda column: gather_of(column).start())
+    each(bcols, col_id, -1, lambda column: gather_of(column, refs["brick"].at[0]).start())
     each(bcols, col_id, -1, lambda column: greet(by_column, column_peer(column)))
     each(brows, row_id, -1, lambda row: greet(by_row, row_peer(row)))
 
@@ -337,7 +337,8 @@
     tabulate()
     find(0, share // 2)
     expect(by_column, bcols - 1 - col_id)
-    each(bcols, col_id, 1, lambda column: gather_of(column).start())
+    own.wait()
+    each(bcols, col_id, 1, lambda column: gather_of(column, pencils.at[col_id]).start())
     find(share // 2, share)
     expect(by_row, brows - 1 - row_id)
 
@@ -395,17 +396,16 @@
                     turn_of(partners[step], turn).start()
 
     groups = [list(range(first, first + batch)) for first in range(0, orients, batch)]
-    own.wait()
+    for name in ("forward", "smoothing", "inverse"):
+        copies[name].wait()
+    both = dot_short(pencils[col_id], refs["forward"][col_id])
     for step in range(1, bcols):
         column = lax.rem(col_id + step, bcols)
         arrived = pencils.at[column]
         pltpu.make_async_copy(arrived, arrived, gather_sems.at[column]).wait()
-    for name in ("forward", "smoothing", "inverse"):
-        copies[name].wait()
-    both = None
-    for part in range(bcols):
-        term = dot_short(pencils[part], refs["forward"][part])
-        both = term if both is None else both + term
+    for step in range(1, bcols):
+        column = lax.rem(col_id + step, bcols)
+        both = both + dot_short(pencils[column], refs["forward"][column])
     padded = both.shape[1] // 2
     real, imag = both[:, :padded], both[:, padded:]
     weights = lax.rsqrt(dot_short(real * real + imag * imag, refs["smoothing"][...]) + epsilon)
@@ -508,8 +508,8 @@
         forward(steps)
     transform(groups[0])
     for steps in groups[1:]:
+        spread(steps)
         unfold(steps)
-        spread(steps)
         transform(steps)
 
     bunch = math.gcd(orients, 8)

time: 16.3 us -> 15.8 us (0.969)
  Pallas kernels: 15.6 us -> 15.1 us
    pallas_call x1, Pallas kernels: 15.6 us -> 15.1 us  [shards(): pl.pallas_call(lambda *refs: staged(sizes, *refs), out_shape=(pltpu.VMEM(...]
where the time goes in v6:
time: 15.8 us; the launch traced here: 15.7 us
  Pallas kernels  15.1 us (96%)
  other arithmetic  0.61 us (4%)
    pallas_call x1, Pallas kernels, shards(): pl.pallas_call(lambda *refs: staged(sizes, *refs), out_shape=(pltpu.VMEM(...  15.1 us
    mul x1, other arithmetic, shards(): return best * scaling  0.61 us

profile of v6, /device:TPU:0, one launch (start us, length us, event | category | flops | bytes accessed | tf_op | source)
XLA Modules:
  0.0 15.7 jit_solution(9731371891633351666)
XLA Ops:
  0.0 15.1 %match.1 = (f32[1,32,104]{2,1,0:T(8,128)S(1)}, f32[1,32,104]{2,1,0:T(8,128)S(1)}) custom-call(f32[1,32,104]{2,1,0:T(8,128)} %refs_0_.1, f32[576,24]{1,0:T(8,128)} %bitcast.1, s32[1,13824]{1,0:T(1,128)} %refs_2_.1, f32[2,104,256]{2,1,0:T(8,128)} %constant.20.clone.refs_3_, f32[128,128]{1,0:T(8,128)} %constant.21.clone.refs_4_, ...), custom_call_target="tpu_custom_call" | custom-call | tf_op jit(solution)/shard_map/match/pallas_call | solution.py:638
  15.1 0.6 %mul.3 = f32[1,32,104]{2,1,0:T(8,128)} multiply(f32[1,32,104]{2,1,0:T(8,128)S(1)} %get-tuple-element.7, f32[1,32,104]{2,1,0:T(8,128)S(1)} %get-tuple-element.8) | non-fusion elementwise | flops 3328 | bytes 39936 | tf_op jit(solution)/shard_map/mul | solution.py:670

commit v7 on v6

--- a/solution.py
+++ b/solution.py
@@ -18,6 +18,12 @@
     return -(-value // step) * step
 
 
+def split(table):
+    upper = table.astype(jnp.bfloat16)
+    lower = (table - upper.astype(np.float64)).astype(jnp.bfloat16)
+    return upper, lower
+
+
 def forward_table(length, parts):
     half = length // 2 + 1
     padded = round_up(half, LANES)
@@ -25,7 +31,7 @@
     table = np.zeros((length, 2 * padded))
     table[:, :half] = np.cos(angles)
     table[:, padded : padded + half] = -np.sin(angles)
-    return table.reshape(parts, length // parts, 2 * padded).astype(np.float32)
+    return np.stack(split(table.reshape(parts, length // parts, 2 * padded)))
 
 
 def smoothing_table(length):
@@ -38,7 +44,7 @@
             table[fold[(k + shift) % length], k] += 1.0 / 3.0
         for other in range(length):
             table[fold[other], k] += floor_share / length
-    return table.astype(np.float32)
+    return np.stack(split(table))
 
 
 def windowed_inverse(length, parts, margin):
@@ -54,13 +60,7 @@
         angles = 2.0 * np.pi * (np.outer(k, columns) % length) / length
         tables[part, :half] = share * np.cos(angles) * inside
         tables[part, padded : padded + half] = -share * np.sin(angles) * inside
-    return tables.astype(np.float32)
-
-
-def split(table):
-    upper = table.astype(jnp.bfloat16)
-    lower = (table - upper.astype(np.float64)).astype(jnp.bfloat16)
-    return upper, lower
+    return np.stack(split(tables))
 
 
 def left_table(table):
@@ -161,6 +161,11 @@
 def by_table(x, table):
     upper, lower = halves(x)
     return product(jnp.concatenate([upper, lower, upper], axis=1), table)
+
+
+def by_halves(x, upper, lower):
+    high, low = halves(x)
+    return product(high, upper) + (product(low, upper) + product(high, lower))
 
 
 def table_by(table, x):
@@ -180,7 +185,7 @@
     pencils,
     windows,
     energy,
-    scores,
+    totals,
     normed,
     table,
     stats,
@@ -398,20 +403,25 @@
     groups = [list(range(first, first + batch)) for first in range(0, orients, batch)]
     for name in ("forward", "smoothing", "inverse"):
         copies[name].wait()
-    both = dot_short(pencils[col_id], refs["forward"][col_id])
+
+    def wave(column):
+        return by_halves(pencils[column], refs["forward"][0, column], refs["forward"][1, column])
+
+    both = wave(col_id)
     for step in range(1, bcols):
         column = lax.rem(col_id + step, bcols)
         arrived = pencils.at[column]
         pltpu.make_async_copy(arrived, arrived, gather_sems.at[column]).wait()
     for step in range(1, bcols):
-        column = lax.rem(col_id + step, bcols)
-        both = both + dot_short(pencils[column], refs["forward"][column])
+        both = both + wave(lax.rem(col_id + step, bcols))
     padded = both.shape[1] // 2
     real, imag = both[:, :padded], both[:, padded:]
-    weights = lax.rsqrt(dot_short(real * real + imag * imag, refs["smoothing"][...]) + epsilon)
-    windows[me, margin : margin + rows] = dot_short(
-        real * weights, refs["inverse"][col_id, :padded, :]
-    ) + dot_short(imag * weights, refs["inverse"][col_id, padded:, :])
+    power = real * real + imag * imag
+    weights = lax.rsqrt(by_halves(power, refs["smoothing"][0], refs["smoothing"][1]) + epsilon)
+    white = both * jnp.concatenate([weights, weights], axis=1)
+    windows[me, margin : margin + rows] = by_halves(
+        white, refs["inverse"][0, col_id], refs["inverse"][1, col_id]
+    )
 
     def window_of(plane):
         part = windows.at[me, pl.ds(margin, rows)]
@@ -441,6 +451,14 @@
         margin_of(me).start()
     for name in tables:
         copies[name].wait()
+
+    def normalise():
+        summed = energy[0:rows, :]
+        for b in range(1, edge):
+            summed = summed + energy[b : b + rows, :]
+        upper, lower = halves(summed)
+        boxed = product(upper, refs["box"][...]) + product(lower, refs["box"][...])
+        scaling_ref[0] = lax.rsqrt(boxed / edge**3 + epsilon)
 
     def transform(steps):
         tiles = []
@@ -455,6 +473,8 @@
             energy[...] += tile * tile * near
             tiles.append(tile)
         turned = by_table(jnp.concatenate(tiles, axis=0), refs["volume_lines"][...])
+        if steps is groups[-1]:
+            normalise()
         for first in range(0, len(steps), 2):
             pair = []
             for i in range(first, first + 2):
@@ -476,7 +496,7 @@
             pieces += [planes[:, j * width : j * width + LANES] for j in range(strips)]
         turned = by_table(jnp.concatenate(pieces, axis=0), refs["template_lines"][...])
         for k in range(2 * span):
-            lines[k] = turned[:, k * size : (k + 1) * size]
+            lines[k, : turned.shape[0]] = turned[:, k * size : (k + 1) * size]
         for i, step in enumerate(steps):
             for first in range(0, orients, 2):
                 pair = [
@@ -502,59 +522,62 @@
     expect(by_far, far)
     send(share_of, "far")
     send(window_of, "far")
+    bunch = math.gcd(orients, 8)
+
+    def rounds(do):
+        if orients == bunch:
+            do(0)
+        else:
+            pl.loop(0, orients // bunch)(lambda i: do(i * bunch))
+
+    def combine(steps, lowest, more):
+        for first in range(0, bunch, 2):
+            for half in range(tile_rows // 8):
+                top = pl.ds(half * 8, 8)
+                low = pl.ds(tile_rows + half * 8, 8)
+                for rotation in (lowest + first, lowest + first + 1):
+                    straight = totals[rotation, top, :] if more else None
+                    crossed = totals[rotation, low, :] if more else None
+                    for step in steps:
+                        plane = partners[step]
+                        wave = templates[rotation, plane, top, :]
+                        term = volumes[plane, top, :] * wave
+                        turn = volumes[plane, low, :] * wave
+                        straight = term if straight is None else straight + term
+                        crossed = turn if crossed is None else crossed + turn
+                    totals[rotation, top, :] = straight
+                    totals[rotation, low, :] = crossed
+
+    def finish(lowest, best):
+        turned = []
+        for first in range(0, bunch, 2):
+            pair = jnp.concatenate([totals[lowest + first], totals[lowest + first + 1]], axis=1)
+            turned.append(table_by(refs["score_rows"][...], pair))
+        for part in turned:
+            halved = [part[:, i * size : (i + 1) * size] for i in range(2)]
+            waves = [jnp.concatenate([half[:rows], half[rows:]], axis=1) for half in halved]
+            scored = by_table(jnp.concatenate(waves, axis=0), refs["score_lines"][...])
+            found = jnp.maximum(scored[:rows], scored[rows:])
+            best = found if best is None else jnp.maximum(best, found)
+        return best
+
     unfold(groups[0])
     spread(groups[0])
     for steps in groups[1:]:
         forward(steps)
     transform(groups[0])
     for steps in groups[1:]:
+        unfold(steps[: batch // 2])
         spread(steps)
-        unfold(steps)
-        transform(steps)
-
-    bunch = math.gcd(orients, 8)
-
-    def combine(lowest):
-        def gather(held, start):
-            held = list(held)
-            for i in range(bunch):
-                straight = volumes[start + i, :tile_rows, :]
-                crossed = volumes[start + i, tile_rows:, :]
-                for j in range(2):
-                    wave = templates[lowest + j, start + i]
-                    held[2 * j] = held[2 * j] + straight * wave
-                    held[2 * j + 1] = held[2 * j + 1] + crossed * wave
-            return tuple(held)
-
-        held = (jnp.zeros((tile_rows, size), jnp.float32),) * 4
-        if orients == bunch:
-            held = gather(held, 0)
-        else:
-            held = lax.fori_loop(0, orients // bunch, lambda i, h: gather(h, i * bunch), held)
-        return jnp.concatenate([jnp.concatenate(held[:2], axis=0), jnp.concatenate(held[2:], axis=0)], axis=1)
-
-    def finish(lowest):
-        for first in range(0, bunch, 2):
-            turned = table_by(refs["score_rows"][...], combine(lowest + first))
-            for i in range(2):
-                part = turned[:, i * size : (i + 1) * size]
-                start = pl.multiple_of((lowest + first + i) * rows, rows)
-                scores[pl.ds(start, rows), :size] = part[:rows]
-                scores[pl.ds(start, rows), size:] = part[rows:]
-
-    if orients == bunch:
-        finish(0)
-    else:
-        pl.loop(0, orients // bunch)(lambda i: finish(i * bunch))
-
-    summed = energy[0:rows, :]
-    for b in range(1, edge):
-        summed = summed + energy[b : b + rows, :]
-    upper, lower = halves(summed)
-    boxed = product(upper, refs["box"][...]) + product(lower, refs["box"][...])
-    scaling_ref[0] = lax.rsqrt(boxed / edge**3 + epsilon)
-    scored = by_table(scores[...], refs["score_lines"][...])
-    best_ref[0] = jnp.max(scored.reshape(orients, rows, cols), axis=0)
+        unfold(steps[batch // 2 :])
+    for i, steps in enumerate(groups):
+        if i:
+            transform(steps)
+        rounds(lambda lowest: combine(steps, lowest, i > 0))
+    best = finish(0, None)
+    if orients > bunch:
+        best = lax.fori_loop(1, orients // bunch, lambda i, best: finish(i * bunch, best), best)
+    best_ref[0] = best
     sent = [
         pencils.at[pl.ds(0, bcols - 1)],
         rotations.at[pl.ds(0, orients - 1), pl.ds(0, share)],
@@ -566,10 +589,6 @@
     for i, ref in enumerate(sent):
         if wanted[i]:
             pltpu.make_async_copy(ref, ref, send_sems.at[i]).wait()
-
-
-def dot_short(a, b):
-    return jnp.dot(a, b, precision=lax.Precision.HIGH, preferred_element_type=jnp.float32)
 
 
 names = (
@@ -650,7 +669,7 @@
             pltpu.VMEM((bcols, rows, cols), jnp.float32),
             pltpu.VMEM((orients, rows + 2 * margin, size), jnp.float32),
             pltpu.VMEM((tile_rows, size), jnp.float32),
-            pltpu.VMEM((orients * rows, 2 * size), jnp.float32),
+            pltpu.VMEM((orients, 2 * tile_rows, size), jnp.float32),
             pltpu.VMEM((edge * edge, edge), jnp.float32),
             pltpu.VMEM((2 * round_up(edge * edge // 8, 16), 8 * edge), jnp.bfloat16),
             pltpu.VMEM((8, LANES), jnp.float32),

time: 15.8 us -> 15.9 us (level)
  no operation moved by 1% of the time
where the time goes in v7:
time: 15.9 us; the launch traced here: 15.8 us
  Pallas kernels  15.2 us (96%)
  other arithmetic  0.61 us (4%)
    pallas_call x1, Pallas kernels, shards(): pl.pallas_call(lambda *refs: staged(sizes, *refs), out_shape=(pltpu.VMEM(...  15.2 us
    mul x1, other arithmetic, shards(): return best * scaling  0.61 us

profile of v7, /device:TPU:0, one launch (start us, length us, event | category | flops | bytes accessed | tf_op | source)
XLA Modules:
  0.0 15.8 jit_solution(15965361853188551290)
XLA Ops:
  0.0 15.2 %match.1 = (f32[1,32,104]{2,1,0:T(8,128)S(1)}, f32[1,32,104]{2,1,0:T(8,128)S(1)}) custom-call(f32[1,32,104]{2,1,0:T(8,128)} %refs_0_.1, f32[576,24]{1,0:T(8,128)} %bitcast.1, s32[1,13824]{1,0:T(1,128)} %refs_2_.1, bf16[2,2,104,256]{3,2,1,0:T(8,128)(2,1)} %constant.20.clone.refs_3_, bf16[2,128,128]{2,1,0:T(8,128)(2,1)} %constant.21.clone.refs_4_, ...), custom_call_target="tpu_custom_call" | custom-call | tf_op jit(solution)/shard_map/match/pallas_call | solution.py:657
  15.2 0.6 %mul.3 = f32[1,32,104]{2,1,0:T(8,128)} multiply(f32[1,32,104]{2,1,0:T(8,128)S(1)} %get-tuple-element.7, f32[1,32,104]{2,1,0:T(8,128)S(1)} %get-tuple-element.8) | non-fusion elementwise | flops 3328 | bytes 39936 | tf_op jit(solution)/shard_map/mul | solution.py:689

commit v8 on v7

--- a/solution.py
+++ b/solution.py
@@ -567,8 +567,9 @@
         forward(steps)
     transform(groups[0])
     for steps in groups[1:]:
+        pl.when(row_id == brows - 1)(lambda: spread(steps))
         unfold(steps[: batch // 2])
-        spread(steps)
+        pl.when(row_id < brows - 1)(lambda: spread(steps))
         unfold(steps[batch // 2 :])
     for i, steps in enumerate(groups):
         if i:

time: 15.9 us -> 15.5 us (0.975)
  Pallas kernels: 15.2 us -> 14.8 us
    pallas_call x1, Pallas kernels: 15.2 us -> 14.8 us  [shards(): pl.pallas_call(lambda *refs: staged(sizes, *refs), out_shape=(pltpu.VMEM(...]
where the time goes in v8:
time: 15.5 us; the launch traced here: 15.4 us
  Pallas kernels  14.8 us (95%)
  other arithmetic  0.61 us (4%)
    pallas_call x1, Pallas kernels, shards(): pl.pallas_call(lambda *refs: staged(sizes, *refs), out_shape=(pltpu.VMEM(...  14.8 us
    mul x1, other arithmetic, shards(): return best * scaling  0.61 us

profile of v8, /device:TPU:0, one launch (start us, length us, event | category | flops | bytes accessed | tf_op | source)
XLA Modules:
  0.0 15.4 jit_solution(9987627929539529434)
XLA Ops:
  0.0 14.8 %match.1 = (f32[1,32,104]{2,1,0:T(8,128)S(1)}, f32[1,32,104]{2,1,0:T(8,128)S(1)}) custom-call(f32[1,32,104]{2,1,0:T(8,128)} %refs_0_.1, f32[576,24]{1,0:T(8,128)} %bitcast.1, s32[1,13824]{1,0:T(1,128)} %refs_2_.1, bf16[2,2,104,256]{3,2,1,0:T(8,128)(2,1)} %constant.20.clone.refs_3_, bf16[2,128,128]{2,1,0:T(8,128)(2,1)} %constant.21.clone.refs_4_, ...), custom_call_target="tpu_custom_call" | custom-call | tf_op jit(solution)/shard_map/match/pallas_call | solution.py:658
  14.8 0.6 %mul.3 = f32[1,32,104]{2,1,0:T(8,128)} multiply(f32[1,32,104]{2,1,0:T(8,128)S(1)} %get-tuple-element.7, f32[1,32,104]{2,1,0:T(8,128)S(1)} %get-tuple-element.8) | non-fusion elementwise | flops 3328 | bytes 39936 | tf_op jit(solution)/shard_map/mul | solution.py:690

commit v9 on v8

--- a/solution.py
+++ b/solution.py
@@ -562,15 +562,15 @@
         return best
 
     unfold(groups[0])
+    for steps in groups[1:]:
+        forward(steps)
     spread(groups[0])
     for steps in groups[1:]:
-        forward(steps)
+        unfold(steps)
+        pl.when(row_id == brows - 1)(lambda: spread(steps))
     transform(groups[0])
     for steps in groups[1:]:
-        pl.when(row_id == brows - 1)(lambda: spread(steps))
-        unfold(steps[: batch // 2])
         pl.when(row_id < brows - 1)(lambda: spread(steps))
-        unfold(steps[batch // 2 :])
     for i, steps in enumerate(groups):
         if i:
             transform(steps)

time: 15.5 us -> 15.5 us (level)
  no operation moved by 1% of the time
where the time goes in v9:
time: 15.5 us; the launch traced here: 15.3 us
  Pallas kernels  14.7 us (95%)
  other arithmetic  0.61 us (4%)
    pallas_call x1, Pallas kernels, shards(): pl.pallas_call(lambda *refs: staged(sizes, *refs), out_shape=(pltpu.VMEM(...  14.7 us
    mul x1, other arithmetic, shards(): return best * scaling  0.61 us

profile of v9, /device:TPU:0, one launch (start us, length us, event | category | flops | bytes accessed | tf_op | source)
XLA Modules:
  0.0 15.3 jit_solution(16046843633875386056)
XLA Ops:
  0.0 14.7 %match.1 = (f32[1,32,104]{2,1,0:T(8,128)S(1)}, f32[1,32,104]{2,1,0:T(8,128)S(1)}) custom-call(f32[1,32,104]{2,1,0:T(8,128)} %refs_0_.1, f32[576,24]{1,0:T(8,128)} %bitcast.1, s32[1,13824]{1,0:T(1,128)} %refs_2_.1, bf16[2,2,104,256]{3,2,1,0:T(8,128)(2,1)} %constant.20.clone.refs_3_, bf16[2,128,128]{2,1,0:T(8,128)(2,1)} %constant.21.clone.refs_4_, ...), custom_call_target="tpu_custom_call" | custom-call | tf_op jit(solution)/shard_map/match/pallas_call | solution.py:658
  14.7 0.6 %mul.3 = f32[1,32,104]{2,1,0:T(8,128)} multiply(f32[1,32,104]{2,1,0:T(8,128)S(1)} %get-tuple-element.7, f32[1,32,104]{2,1,0:T(8,128)S(1)} %get-tuple-element.8) | non-fusion elementwise | flops 3328 | bytes 39936 | tf_op jit(solution)/shard_map/mul | solution.py:690

commit v10 on v9

--- a/solution.py
+++ b/solution.py
@@ -345,7 +345,6 @@
     own.wait()
     each(bcols, col_id, 1, lambda column: gather_of(column, pencils.at[col_id]).start())
     find(share // 2, share)
-    expect(by_row, brows - 1 - row_id)
 
     def block(rotation, part):
         return rotations.at[rotation, pl.ds(part * share, share)]
@@ -360,23 +359,25 @@
             device_id_type=MESH,
         )
 
-    def turn_of(rotation, turn):
+    def turn_of(step, turn):
+        rotation = partners[step]
         row = lax.rem(row_id + turn, brows)
         return pltpu.make_async_remote_copy(
             src_ref=block(rotation, mine),
             dst_ref=block(rotation, mine),
             send_sem=send_sems.at[2],
-            recv_sem=turn_sems.at[rotation],
+            recv_sem=turn_sems.at[step // batch],
             device_id=row_peer(row),
             device_id_type=MESH,
         )
 
-    rotations[me, pl.ds(mine * share, share)] = rotated[pl.ds(first_of(mine, me), share)]
-    for turn in range(1, parts):
-        turn_of(me, turn).start()
     expect(by_pair, 1 - odd)
     each(orients, me, -1, lambda plane: share_of(plane).start())
     pl.when(odd == 0)(lambda: share_of(me + 1).start())
+    expect(by_row, brows - 1 - row_id)
+    rotations[me, pl.ds(mine * share, share)] = rotated[pl.ds(first_of(mine, me), share)]
+    for turn in range(1, parts):
+        turn_of(0, turn).start()
     near = (2 * last - pair) // (last + 1)
     far = last - pair - near
 
@@ -398,7 +399,7 @@
                 arrived = block(partners[step], mine)
                 pltpu.make_async_copy(arrived, arrived, share_sems.at[partners[step]]).wait()
                 for turn in range(1, parts):
-                    turn_of(partners[step], turn).start()
+                    turn_of(step, turn).start()
 
     groups = [list(range(first, first + batch)) for first in range(0, orients, batch)]
     for name in ("forward", "smoothing", "inverse"):
@@ -434,12 +435,13 @@
             device_id_type=MESH,
         )
 
-    def margin_of(plane):
+    def margin_of(step):
+        plane = partners[step]
         return pltpu.make_async_remote_copy(
             src_ref=windows.at[plane, pl.ds(pl.multiple_of(rows - row_id * (rows - margin), 8), margin)],
             dst_ref=windows.at[plane, pl.ds(pl.multiple_of(row_id * (margin + rows), 8), margin)],
             send_sem=send_sems.at[4],
-            recv_sem=margin_sems.at[plane],
+            recv_sem=margin_sems.at[step // batch],
             device_id=row_peer(lax.rem(row_id + 1, brows)),
             device_id_type=MESH,
         )
@@ -448,7 +450,7 @@
     pl.when(odd == 0)(lambda: window_of(me + 1).start())
     send(window_of, "near")
     if brows > 1:
-        margin_of(me).start()
+        margin_of(0).start()
     for name in tables:
         copies[name].wait()
 
@@ -461,12 +463,12 @@
         scaling_ref[0] = lax.rsqrt(boxed / edge**3 + epsilon)
 
     def transform(steps):
+        if brows > 1:
+            arrived = windows.at[pl.ds(0, batch), pl.ds(0, margin)]
+            pltpu.make_async_copy(arrived, arrived, margin_sems.at[steps[0] // batch]).wait()
         tiles = []
         for step in steps:
             plane = partners[step]
-            if brows > 1:
-                arrived = windows.at[plane, pl.ds(0, margin)]
-                pltpu.make_async_copy(arrived, arrived, margin_sems.at[plane]).wait()
             tile = windows[plane, skip : skip + tile_rows]
             gap = plane - me
             near = jnp.logical_and(gap >= -half_edge, gap < half_edge).astype(jnp.float32)
@@ -485,10 +487,9 @@
                 volumes[partners[steps[first + i]]] = spun[:, i * size : (i + 1) * size]
 
     def unfold(steps):
-        for step in steps:
-            if parts > 1:
-                arrived = rotations.at[partners[step], pl.ds(0, orients - share)]
-                pltpu.make_async_copy(arrived, arrived, turn_sems.at[partners[step]]).wait()
+        if parts > 1:
+            arrived = rotations.at[pl.ds(0, batch), pl.ds(0, orients - share)]
+            pltpu.make_async_copy(arrived, arrived, turn_sems.at[steps[0] // batch]).wait()
         width = span * edge
         pieces = []
         for step in steps:
@@ -516,7 +517,7 @@
                 arrived = windows.at[partners[step], pl.ds(margin, rows)]
                 pltpu.make_async_copy(arrived, arrived, window_sems.at[partners[step]]).wait()
                 if brows > 1:
-                    margin_of(partners[step]).start()
+                    margin_of(step).start()
 
     forward(groups[0])
     expect(by_far, far)
@@ -677,9 +678,9 @@
             pltpu.SemaphoreType.DMA,
             pltpu.SemaphoreType.DMA((bcols,)),
             pltpu.SemaphoreType.DMA((orients,)),
+            pltpu.SemaphoreType.DMA((orients // batch,)),
             pltpu.SemaphoreType.DMA((orients,)),
-            pltpu.SemaphoreType.DMA((orients,)),
-            pltpu.SemaphoreType.DMA((orients,)),
+            pltpu.SemaphoreType.DMA((orients // batch,)),
             pltpu.SemaphoreType.DMA((5,)),
             pltpu.SemaphoreType.REGULAR((5,)),
             pltpu.SemaphoreType.DMA((len(names),)),

time: 15.5 us -> 15.4 us (level)
  no operation moved by 1% of the time
where the time goes in v10:
time: 15.4 us; the launch traced here: 15.2 us
  Pallas kernels  14.6 us (95%)
  other arithmetic  0.61 us (4%)
    pallas_call x1, Pallas kernels, shards(): pl.pallas_call(lambda *refs: staged(sizes, *refs), out_shape=(pltpu.VMEM(...  14.6 us
    mul x1, other arithmetic, shards(): return best * scaling  0.61 us

profile of v10, /device:TPU:0, one launch (start us, length us, event | category | flops | bytes accessed | tf_op | source)
XLA Modules:
  0.0 15.2 jit_solution(14128268982887377049)
XLA Ops:
  0.0 14.6 %match.1 = (f32[1,32,104]{2,1,0:T(8,128)S(1)}, f32[1,32,104]{2,1,0:T(8,128)S(1)}) custom-call(f32[1,32,104]{2,1,0:T(8,128)} %refs_0_.1, f32[576,24]{1,0:T(8,128)} %bitcast.1, s32[1,13824]{1,0:T(1,128)} %refs_2_.1, bf16[2,2,104,256]{3,2,1,0:T(8,128)(2,1)} %constant.20.clone.refs_3_, bf16[2,128,128]{2,1,0:T(8,128)(2,1)} %constant.21.clone.refs_4_, ...), custom_call_target="tpu_custom_call" | custom-call | tf_op jit(solution)/shard_map/match/pallas_call | solution.py:659
  14.6 0.6 %mul.3 = f32[1,32,104]{2,1,0:T(8,128)} multiply(f32[1,32,104]{2,1,0:T(8,128)S(1)} %get-tuple-element.7, f32[1,32,104]{2,1,0:T(8,128)S(1)} %get-tuple-element.8) | non-fusion elementwise | flops 3328 | bytes 39936 | tf_op jit(solution)/shard_map/mul | solution.py:691

commit v11 on v10

--- a/solution.py
+++ b/solution.py
@@ -258,6 +258,10 @@
         found = first_of(part, me) + index
         return found // 2 * (2 * parts) + 2 * part + lax.rem(found, 2) - orients + me
 
+    tables = ("template_lines", "template_rows", "volume_lines", "volume_rows", "score_rows", "score_lines", "box")
+    for name, copy in copies.items():
+        if name not in tables:
+            copy.start()
     windows[...] = jnp.zeros_like(windows)
     barrier = pltpu.get_barrier_semaphore()
     @pl.when(odd == 0)
@@ -270,10 +274,6 @@
 
     each(bcols, col_id, 1, lambda column: greet(barrier, column_peer(column)))
     each(brows, row_id, 1, lambda row: greet(barrier, row_peer(row)))
-    tables = ("template_lines", "template_rows", "volume_lines", "volume_rows", "score_rows", "score_lines", "box")
-    for name, copy in copies.items():
-        if name not in tables:
-            copy.start()
     own = pltpu.make_async_copy(refs["brick"].at[0], pencils.at[col_id], own_sem)
     own.start()
     energy[...] = jnp.zeros_like(energy)

time: 15.4 us -> 15.3 us (level)
  no operation moved by 1% of the time
where the time goes in v11:
time: 15.3 us; the launch traced here: 15.2 us
  Pallas kernels  14.5 us (95%)
  other arithmetic  0.61 us (4%)
    pallas_call x1, Pallas kernels, shards(): pl.pallas_call(lambda *refs: staged(sizes, *refs), out_shape=(pltpu.VMEM(...  14.5 us
    mul x1, other arithmetic, shards(): return best * scaling  0.61 us

profile of v11, /device:TPU:0, one launch (start us, length us, event | category | flops | bytes accessed | tf_op | source)
XLA Modules:
  0.0 15.2 jit_solution(18430928732435608443)
XLA Ops:
  0.0 14.5 %match.1 = (f32[1,32,104]{2,1,0:T(8,128)S(1)}, f32[1,32,104]{2,1,0:T(8,128)S(1)}) custom-call(f32[1,32,104]{2,1,0:T(8,128)} %refs_0_.1, f32[576,24]{1,0:T(8,128)} %bitcast.1, s32[1,13824]{1,0:T(1,128)} %refs_2_.1, bf16[2,2,104,256]{3,2,1,0:T(8,128)(2,1)} %constant.20.clone.refs_3_, bf16[2,128,128]{2,1,0:T(8,128)(2,1)} %constant.21.clone.refs_4_, ...), custom_call_target="tpu_custom_call" | custom-call | tf_op jit(solution)/shard_map/match/pallas_call | solution.py:659
  14.5 0.6 %mul.3 = f32[1,32,104]{2,1,0:T(8,128)} multiply(f32[1,32,104]{2,1,0:T(8,128)S(1)} %get-tuple-element.7, f32[1,32,104]{2,1,0:T(8,128)S(1)} %get-tuple-element.8) | non-fusion elementwise | flops 3328 | bytes 39936 | tf_op jit(solution)/shard_map/mul | solution.py:691
